TPU v7x, 512 devices: a whole 4x8x8 slice. The times are simulated.
512 devices in a mesh: ctx: 16 (over y, core), chan: 32 (over z, x).
Axes of the slice: x: 4, y: 8, z: 8, core: 2. Of those that a mesh axis runs over, the one named last changes fastest.
Arguments:
- out_gate: bfloat16 [512, 16384], P('chan', 'ctx'), may hold values from -6 to 6
- in_gate: bfloat16 [512, 16384], P('chan', 'ctx'), may hold values from -6 to 6
- signal: bfloat16 [512, 16384], P('chan', 'ctx'), may hold values from -6 to 6
- grad_out: bfloat16 [512, 16384], P('chan', 'ctx'), may hold values from -6 to 6
- position_table: float32 [33, 16384], P(None, 'ctx'), may hold values from -6 to 6
- embed_weight: float32 [33, 64], replicated, may hold values from -1 to 1
- hidden_weight: float32 [64, 64], replicated, may hold values from -0.75 to 0.75
- filter_weight: float32 [64, 512], P(None, 'chan'), may hold values from -0.75 to 0.75
- decay_rate: float32 [512], P('chan'), may hold values from 0 to 1, as said below
- skip_gain: float32 [512], P('chan'), may hold values from -6 to 6
Outputs:
- mixed: bfloat16 [512, 16384], P('chan', 'ctx')
- out_gate_grad: bfloat16 [512, 16384], P('chan', 'ctx')
- in_gate_grad: bfloat16 [512, 16384], P('chan', 'ctx')
- signal_grad: bfloat16 [512, 16384], P('chan', 'ctx')
- embed_weight_grad: float32 [33, 64], replicated
- hidden_weight_grad: float32 [64, 64], replicated
- filter_weight_grad: float32 [64, 512], P(None, 'chan')
- skip_gain_grad: float32 [512], P('chan')
- position_grad: float32 [33, 16384], P(None, 'ctx')
Inputs may be any that keep to these rules, and one draw needn't show every extreme that they name: `decay_rate`: positive decay rates; some channels keep their filter over the whole sequence, the others decay with e-fold lengths from about 30 positions to a large fraction of the sequence.
All inputs are finite; a program needn't handle non-finite values.
Results may differ from a plain program's by a relative error of at most 0.0013.
Values sent between devices are 32-bit elements; how exact they have to be, the bound alone decides.
A program may use at most 64 MiB of HBM per device.

v0:
```python
import math

import jax
import jax.numpy as jnp
from jax import lax
from jax.sharding import PartitionSpec as P

EPSILON = 1e-06
PRECISE = lax.Precision.HIGHEST


def partner_2(block, axis, distance):
    count = lax.axis_size(axis)
    route = []
    for low in range(count):
        high = low | 1 << distance
        if high != low and high < count:
            route += [(low, high), (high, low)]
    return lax.ppermute(block, axis, route)


def matmul(left_side, right_side):
    return jnp.dot(left_side, right_side, precision=PRECISE, preferred_element_type=jnp.float32)


def phase_table(row_count, col_count, period, sign_value):
    row_ids = lax.broadcasted_iota(jnp.int32, (row_count, col_count), 0)
    col_ids = lax.broadcasted_iota(jnp.int32, (row_count, col_count), 1)
    phase_angle = (
        sign_value * 2.0 * math.pi / period * (row_ids * col_ids % period).astype(jnp.float32)
    )
    return (jnp.cos(phase_angle), jnp.sin(phase_angle))


def block_table(order_len, sign_value):
    cosine, sine_part = phase_table(order_len, order_len, order_len, sign_value)
    return jnp.stack(
        [jnp.stack([cosine, -sine_part], axis=1), jnp.stack([sine_part, cosine], axis=1)], axis=0
    )


def rotate_pair(current, cosine, sine_part):
    real_part = current[:, 0] * cosine - current[:, 1] * sine_part
    imag_part = current[:, 0] * sine_part + current[:, 1] * cosine
    return jnp.stack([real_part, imag_part], axis=1)


def split_length(length):
    short_len = 1
    for factor in range(1, math.isqrt(length) + 1):
        if length % factor == 0:
            short_len = factor
    return (short_len, length // short_len)


def local_transform(current, sign_value):
    length = current.shape[-1]
    lead_count = current.shape[0]
    channels = current.shape[2]
    short_len, long_len = split_length(length)
    if sign_value < 0:
        working = current.reshape(lead_count, 2, channels, short_len, long_len)
        working = jnp.einsum(
            "aibj,kbcjl->kacil",
            block_table(short_len, sign_value),
            working,
            precision=PRECISE,
            preferred_element_type=jnp.float32,
        )
        cosine, sine_part = phase_table(short_len, long_len, length, sign_value)
        working = rotate_pair(working, cosine, sine_part)
        working = jnp.einsum(
            "aibj,kbcmj->kacim",
            block_table(long_len, sign_value),
            working,
            precision=PRECISE,
            preferred_element_type=jnp.float32,
        )
    else:
        working = current.reshape(lead_count, 2, channels, long_len, short_len)
        working = jnp.einsum(
            "aibj,kbcjm->kacim",
            block_table(long_len, sign_value),
            working,
            precision=PRECISE,
            preferred_element_type=jnp.float32,
        )
        cosine, sine_part = phase_table(long_len, short_len, length, sign_value)
        working = rotate_pair(working, cosine, sine_part)
        working = jnp.einsum(
            "aibj,kbcsj->kacis",
            block_table(short_len, sign_value),
            working,
            precision=PRECISE,
            preferred_element_type=jnp.float32,
        )
    return working.reshape(lead_count, 2, channels, length)


def reversed_index(own_index, bit_total):
    reversed_sum = jnp.zeros((), jnp.int32)
    for bit_num in range(bit_total):
        reversed_sum = reversed_sum + (own_index >> bit_num & 1) * (1 << bit_total - 1 - bit_num)
    return reversed_sum


def spectrum_start():
    own_index = lax.axis_index("ctx")
    return 2 * reversed_index(own_index, lax.axis_size("ctx").bit_length() - 1)


def apply_twist(current, first_freq, sign_value):
    length = current.shape[-1]
    period = 2 * lax.axis_size("ctx") * length
    freq_ids = first_freq + lax.broadcasted_iota(jnp.int32, (2, 1, length), 0)
    cell_ids = lax.broadcasted_iota(jnp.int32, (2, 1, length), 2)
    phase_angle = (
        sign_value * 2.0 * math.pi / period * (freq_ids * cell_ids % period).astype(jnp.float32)
    )
    return rotate_pair(current, jnp.cos(phase_angle), jnp.sin(phase_angle))


def pairs_forward(field_block):
    ctx_count = lax.axis_size("ctx")
    bit_total = ctx_count.bit_length() - 1
    own_index = lax.axis_index("ctx")
    phase_angle = -math.pi / ctx_count * own_index.astype(jnp.float32)
    zero_part = jnp.zeros_like(field_block)
    current = jnp.stack(
        [
            jnp.stack([field_block, zero_part]),
            jnp.stack([field_block * jnp.cos(phase_angle), field_block * jnp.sin(phase_angle)]),
        ]
    )
    for bit_num in reversed(range(bit_total)):
        half_span = 1 << bit_num
        partner = partner_2(current, "ctx", bit_num)
        is_lower = own_index >> bit_num & 1 == 0
        angle_step = -math.pi / half_span * (own_index % half_span).astype(jnp.float32)
        rotated = rotate_pair(partner - current, jnp.cos(angle_step), jnp.sin(angle_step))
        current = jnp.where(is_lower, current + partner, rotated)
    return current


def pairs_inverse(current):
    ctx_count = lax.axis_size("ctx")
    bit_total = ctx_count.bit_length() - 1
    own_index = lax.axis_index("ctx")
    for bit_num in range(bit_total):
        half_span = 1 << bit_num
        partner = partner_2(current, "ctx", bit_num)
        is_lower = own_index >> bit_num & 1 == 0
        angle_step = math.pi / half_span * (own_index % half_span).astype(jnp.float32)
        cosine = jnp.cos(angle_step)
        sine_part = jnp.sin(angle_step)
        lower_value = current + rotate_pair(partner, cosine, sine_part)
        upper_value = partner - rotate_pair(current, cosine, sine_part)
        current = jnp.where(is_lower, lower_value, upper_value)
    phase_angle = math.pi / ctx_count * own_index.astype(jnp.float32)
    return (
        current[0, 0] + current[1, 0] * jnp.cos(phase_angle) - current[1, 1] * jnp.sin(phase_angle)
    )


def transform(field_block):
    current = pairs_forward(field_block)
    current = apply_twist(current, spectrum_start(), -1.0)
    return local_transform(current, -1.0)


def untransform(spectra):
    current = local_transform(spectra, 1.0)
    current = apply_twist(current, spectrum_start(), 1.0)
    real_field = pairs_inverse(current)
    return real_field * (1.0 / (2 * lax.axis_size("ctx") * spectra.shape[-1]))


def spectral_product(first_spec, second, conjugate):
    first_imag = -first_spec[:, 1] if conjugate else first_spec[:, 1]
    real_part = first_spec[:, 0] * second[:, 0] - first_imag * second[:, 1]
    imag_part = first_spec[:, 0] * second[:, 1] + first_imag * second[:, 0]
    return jnp.stack([real_part, imag_part], axis=1)


def shards(
    out_gate,
    in_gate,
    signal,
    grad_out,
    position_table,
    embed_weight,
    hidden_weight,
    filter_weight,
    decay_rate,
    skip_gain,
):
    length = signal.shape[1]
    grad_scale = (length * lax.axis_size("ctx")) ** (-0.5)
    pre_one = matmul(embed_weight.T, position_table)
    act_one = jnp.sin(pre_one)
    pre_two = matmul(hidden_weight.T, act_one)
    act_two = jnp.sin(pre_two)
    raw_filter = matmul(filter_weight.T, act_two)
    cell_ids = lax.axis_index("ctx") * length + lax.broadcasted_iota(jnp.int32, (1, length), 1)
    envelope = jnp.exp(-decay_rate[:, None] * cell_ids.astype(jnp.float32))
    shaped = raw_filter * envelope
    energy = lax.psum(jnp.sum(shaped * shaped, axis=1), "ctx")
    inverse_norm = lax.rsqrt(energy + EPSILON)
    kernel = shaped * inverse_norm[:, None]
    product = in_gate.astype(jnp.float32) * signal.astype(jnp.float32)
    upstream = grad_out.astype(jnp.float32)
    through = upstream * out_gate.astype(jnp.float32)
    kernel_spec = transform(kernel)
    product_spec = transform(product)
    through_spec = transform(through)
    convolved = untransform(spectral_product(kernel_spec, product_spec, False))
    back_conv = untransform(spectral_product(kernel_spec, through_spec, True))
    kernel_grad = untransform(spectral_product(product_spec, through_spec, True))
    gated_sum = convolved + skip_gain[:, None] * product
    mixed_out = (out_gate.astype(jnp.float32) * gated_sum).astype(jnp.bfloat16)
    out_gate_grad = (upstream * gated_sum).astype(jnp.bfloat16)
    product_grad = back_conv + skip_gain[:, None] * through
    in_gate_grad = (product_grad * signal.astype(jnp.float32)).astype(jnp.bfloat16)
    signal_grad = (product_grad * in_gate.astype(jnp.float32)).astype(jnp.bfloat16)
    along_kernel, skip_sum = lax.psum(
        (jnp.sum(kernel_grad * kernel, axis=1), jnp.sum(through * product, axis=1)), "ctx"
    )
    raw_grad = (kernel_grad - kernel * along_kernel[:, None]) * inverse_norm[:, None] * envelope
    filter_part = matmul(act_two, raw_grad.T)
    act_two_part = matmul(filter_weight, raw_grad)
    act_two_grad = lax.psum(act_two_part, "chan")
    pre_two_grad = act_two_grad * jnp.cos(pre_two)
    act_one_grad = matmul(hidden_weight, pre_two_grad)
    pre_one_grad = act_one_grad * jnp.cos(pre_one)
    position_grad = matmul(embed_weight, pre_one_grad)
    filter_sum, hidden_sum, embed_sum = lax.psum(
        (filter_part, matmul(act_one, pre_two_grad.T), matmul(position_table, pre_one_grad.T)),
        "ctx",
    )
    return (
        mixed_out,
        out_gate_grad,
        in_gate_grad,
        signal_grad,
        embed_sum * grad_scale,
        hidden_sum * grad_scale,
        filter_sum * grad_scale,
        skip_sum * grad_scale,
        position_grad,
    )


def solution(mesh):
    placed = (
        P("chan", "ctx"),
        P("chan", "ctx"),
        P("chan", "ctx"),
        P("chan", "ctx"),
        P(None, "ctx"),
        P(),
        P(),
        P(None, "chan"),
        P("chan"),
        P("chan"),
    )
    return jax.shard_map(
        shards,
        mesh=mesh,
        in_specs=placed,
        out_specs=(
            P("chan", "ctx"),
            P("chan", "ctx"),
            P("chan", "ctx"),
            P("chan", "ctx"),
            P(),
            P(),
            P(None, "chan"),
            P("chan"),
            P(None, "ctx"),
        ),
        check_vma=False,
    )
```

profile of v0, /device:TPU:1, one launch (start us, length us, event | category | flops | bytes accessed | tf_op | source)
XLA Modules:
  0.0 505.4 jit_solution(7949770406502479690)
XLA Ops:
  10.0 2.0 fusion.93
  12.4 29.8 %psum.49 = f32[16]{0:T(128)S(1)} all-reduce(f32[16]{0:T(128)S(1)} %get-tuple-element.162), channel_id=1, replica_groups=mesh['ctx'=16,'chan'=32] {'ctx'}, use_global_device_ids=true, to_apply=%region_1.0 | all-reduce | flops 16 | bytes 128 | tf_op jit(solution)/shard_map/psum | solution.py:207
  42.4 2.1 collective-permute-start
  44.6 7.1 %collective-permute-start.4 = (f32[2,2,16,1024]{3,2,1,0:T(8,128)S(1)}, f32[2,2,16,1024]{3,2,1,0:T(8,128)S(1)}, u32[]{:S(2)}, u32[]{:S(2)}) collective-permute-start(f32[2,2,16,1024]{3,2,1,0:T(8,128)S(1)} %pad_maximum_fusion.1), channel_id=1, source_target_pairs={{0,256},{256,0},{32,288},{288,32},{64,320},{320,64},{96,352},{352,... | collective-permute-start | bytes 786440 | tf_op jit(solution)/shard_map/ppermute | solution.py:19
  51.8 2.1 collective-permute-start.12
  60.8 9.9 %collective-permute-done = f32[2,2,16,1024]{3,2,1,0:T(8,128)S(1)} collective-permute-done((f32[2,2,16,1024]{3,2,1,0:T(8,128)S(1)}, f32[2,2,16,1024]{3,2,1,0:T(8,128)S(1)}, u32[]{:S(2)}, u32[]{:S(2)}) %collective-permute-start) | collective-permute-done | bytes 262176 | tf_op jit(solution)/shard_map/ppermute | solution.py:19
  70.8 1.9 collective-permute-start.1
  72.7 3.6 collective-permute-done.4
  76.5 1.9 collective-permute-start.5
  78.4 3.6 collective-permute-done.12
  82.1 1.9 collective-permute-start.13
  84.0 20.3 %collective-permute-done.1 = f32[2,2,16,1024]{3,2,1,0:T(8,128)S(1)} collective-permute-done((f32[2,2,16,1024]{3,2,1,0:T(8,128)S(1)}, f32[2,2,16,1024]{3,2,1,0:T(8,128)S(1)}, u32[]{:S(2)}, u32[]{:S(2)}) %collective-permute-start.1) | collective-permute-done | bytes 262176 | tf_op jit(solution)/shard_map/ppermute | solution.py:19
  104.5 1.9 collective-permute-start.2
  106.5 3.5 collective-permute-done.5
  110.1 1.9 collective-permute-start.6
  112.1 3.5 collective-permute-done.13
  115.8 1.9 collective-permute-start.14
  117.7 3.4 collective-permute-done.2
  121.3 2.5 collective-permute-start.3
  123.8 3.0 collective-permute-done.6
  126.9 2.5 collective-permute-start.7
  129.4 3.0 collective-permute-done.14
  132.5 2.9 collective-permute-start.15
  150.2 3.0 convolution_bitcast_fusion.8
  154.7 3.2 convolution_bitcast_fusion.4
  174.1 3.0 convolution_bitcast_fusion.2
  178.6 3.2 convolution_bitcast_fusion
  183.5 2.3 collective-permute-start.20
  185.8 2.0 collective-permute-start.8
  187.8 2.3 collective-permute-start.16
  190.3 1.9 collective-permute-start.21
  192.3 3.4 collective-permute-start.9
  195.9 1.9 collective-permute-start.17
  197.8 2.1 collective-permute-done.21
  200.1 1.9 collective-permute-start.22
  202.1 3.5 collective-permute-done.9
  205.7 1.9 collective-permute-start.10
  207.7 8.0 %collective-permute-done.17 = f32[2,2,16,1024]{3,2,1,0:T(8,128)S(1)} collective-permute-done((f32[2,2,16,1024]{3,2,1,0:T(8,128)S(1)}, f32[2,2,16,1024]{3,2,1,0:T(8,128)S(1)}, u32[]{:S(2)}, u32[]{:S(2)}) %collective-permute-start.17) | collective-permute-done | bytes 262176 | tf_op jit(solution)/shard_map/ppermute | solution.py:19
  215.9 3.3 collective-permute-start.18
  219.3 4.1 collective-permute-start.23
  223.5 14.9 %collective-permute-done.10 = f32[2,2,16,1024]{3,2,1,0:T(8,128)S(1)} collective-permute-done((f32[2,2,16,1024]{3,2,1,0:T(8,128)S(1)}, f32[2,2,16,1024]{3,2,1,0:T(8,128)S(1)}, u32[]{:S(2)}, u32[]{:S(2)}) %collective-permute-start.10) | collective-permute-done | bytes 262176 | tf_op jit(solution)/shard_map/ppermute | solution.py:19
  238.4 1.9 collective-permute-start.11
  240.4 12.5 %collective-permute-done.18 = f32[2,2,16,1024]{3,2,1,0:T(8,128)S(1)} collective-permute-done((f32[2,2,16,1024]{3,2,1,0:T(8,128)S(1)}, f32[2,2,16,1024]{3,2,1,0:T(8,128)S(1)}, u32[]{:S(2)}, u32[]{:S(2)}) %collective-permute-start.18) | collective-permute-done | bytes 262176 | tf_op jit(solution)/shard_map/ppermute | solution.py:19
  253.0 1.9 collective-permute-start.19
  255.3 33.7 %psum.50 = f32[16]{0:T(128)S(1)} all-reduce(f32[16]{0:T(128)S(1)} %get-tuple-element.13), channel_id=1, replica_groups=mesh['ctx'=16,'chan'=32] {'ctx'}, use_global_device_ids=true, to_apply=%region_3.4 | all-reduce | flops 16 | bytes 128 | tf_op jit(solution)/shard_map/psum | solution.py:225
  294.2 148.3 %all-reduce.6.cloned.1.call-done = f32[64,1024]{1,0:T(8,128)} async-done(((f32[64,1024]{1,0:T(8,128)}), f32[64,1024]{1,0:T(8,128)}) %all-reduce.6.cloned.1.call-update) | async-done | bytes 262160 | tf_op jit(solution)/shard_map/psum | solution.py:231
  442.5 3.0 fusion
  448.6 47.4 %all-reduce.3 = (f32[33,64]{1,0:T(8,128)S(1)}, f32[64,64]{1,0:T(8,128)S(1)}, f32[64,16]{0,1:T(8,128)S(1)}, f32[16]{0:T(128)S(1)}) all-reduce(f32[33,64]{1,0:T(8,128)S(1)} %convolution_bitcast_fusion.16, f32[64,64]{1,0:T(8,128)S(1)} %fusion.38, f32[64,16]{0,1:T(8,128)S(1)} %fusion.85, ...), channel_id=1, replica_groups=mesh['ctx'=16,'chan'=32] {'ctx'}, use_global_device_ids=true, to_apply=%region_5.6 | all-reduce | flops 7248 | bytes 57984 | tf_op jit(solution)/shard_map/psum | solution.py:236
  (255 shorter events, 57.8 us)
Async XLA Ops:
  7.2 435.3 %all-reduce.6.cloned.1.call-start = ((), (), s32[]{:S(2)}) async-start(), calls=%async_computation | async-start | bytes 524288 | tf_op jit(solution)/shard_map/psum | solution.py:231
  8.1 3.9 copy-start.36
  8.1 1.9 copy-start.22
  10.0 2.0 copy-start.34
  42.3 2.2 copy-start.15
  42.3 2.2 copy-start.16
  42.3 2.2 copy-start.18
  42.3 2.2 copy-start.20
  42.4 28.3 %collective-permute-start = (f32[2,2,16,1024]{3,2,1,0:T(8,128)S(1)}, f32[2,2,16,1024]{3,2,1,0:T(8,128)S(1)}, u32[]{:S(2)}, u32[]{:S(2)}) collective-permute-start(f32[2,2,16,1024]{3,2,1,0:T(8,128)S(1)} %pad_maximum_fusion), channel_id=1, source_target_pairs={{0,256},{256,0},{32,288},{288,32},{64,320},{320,64},{96,352},{352,... | collective-permute-start | bytes 786440 | tf_op jit(solution)/shard_map/ppermute | solution.py:19
  44.6 31.7 %collective-permute-start.4 = (f32[2,2,16,1024]{3,2,1,0:T(8,128)S(1)}, f32[2,2,16,1024]{3,2,1,0:T(8,128)S(1)}, u32[]{:S(2)}, u32[]{:S(2)}) collective-permute-start(f32[2,2,16,1024]{3,2,1,0:T(8,128)S(1)} %pad_maximum_fusion.1), channel_id=1, source_target_pairs={{0,256},{256,0},{32,288},{288,32},{64,320},{320,64},{96,352},{352,... | collective-permute-start | bytes 786440 | tf_op jit(solution)/shard_map/ppermute | solution.py:19
  51.8 30.2 %collective-permute-start.12 = (f32[2,2,16,1024]{3,2,1,0:T(8,128)S(1)}, f32[2,2,16,1024]{3,2,1,0:T(8,128)S(1)}, u32[]{:S(2)}, u32[]{:S(2)}) collective-permute-start(f32[2,2,16,1024]{3,2,1,0:T(8,128)S(1)} %pad_maximum_fusion.3), channel_id=1, source_target_pairs={{0,256},{256,0},{32,288},{288,32},{64,320},{320,64},{96,352},{352,... | collective-permute-start | bytes 786440 | tf_op jit(solution)/shard_map/ppermute | solution.py:19
  70.8 33.5 %collective-permute-start.1 = (f32[2,2,16,1024]{3,2,1,0:T(8,128)S(1)}, f32[2,2,16,1024]{3,2,1,0:T(8,128)S(1)}, u32[]{:S(2)}, u32[]{:S(2)}) collective-permute-start(f32[2,2,16,1024]{3,2,1,0:T(8,128)S(1)} %maximum_select_fusion), channel_id=1, source_target_pairs={{0,128},{128,0},{32,160},{160,32},{64,192},{192,64},{96,224},{224,... | collective-permute-start | bytes 786440 | tf_op jit(solution)/shard_map/ppermute | solution.py:19
  76.5 33.5 %collective-permute-start.5 = (f32[2,2,16,1024]{3,2,1,0:T(8,128)S(1)}, f32[2,2,16,1024]{3,2,1,0:T(8,128)S(1)}, u32[]{:S(2)}, u32[]{:S(2)}) collective-permute-start(f32[2,2,16,1024]{3,2,1,0:T(8,128)S(1)} %maximum_select_fusion.4), channel_id=1, source_target_pairs={{0,128},{128,0},{32,160},{160,32},{64,192},{192,64},{96,224},{224,... | collective-permute-start | bytes 786440 | tf_op jit(solution)/shard_map/ppermute | solution.py:19
  82.1 33.5 %collective-permute-start.13 = (f32[2,2,16,1024]{3,2,1,0:T(8,128)S(1)}, f32[2,2,16,1024]{3,2,1,0:T(8,128)S(1)}, u32[]{:S(2)}, u32[]{:S(2)}) collective-permute-start(f32[2,2,16,1024]{3,2,1,0:T(8,128)S(1)} %maximum_select_fusion.8), channel_id=1, source_target_pairs={{0,128},{128,0},{32,160},{160,32},{64,192},{192,64},{96,224},{224,... | collective-permute-start | bytes 786440 | tf_op jit(solution)/shard_map/ppermute | solution.py:19
  104.5 16.6 %collective-permute-start.2 = (f32[2,2,16,1024]{3,2,1,0:T(8,128)S(1)}, f32[2,2,16,1024]{3,2,1,0:T(8,128)S(1)}, u32[]{:S(2)}, u32[]{:S(2)}) collective-permute-start(f32[2,2,16,1024]{3,2,1,0:T(8,128)S(1)} %maximum_select_fusion.1), channel_id=1, source_target_pairs={{0,64},{64,0},{32,96},{96,32},{128,192},{192,128},{160,224},{224,1... | collective-permute-start | bytes 786440 | tf_op jit(solution)/shard_map/ppermute | solution.py:19
  110.1 16.6 %collective-permute-start.6 = (f32[2,2,16,1024]{3,2,1,0:T(8,128)S(1)}, f32[2,2,16,1024]{3,2,1,0:T(8,128)S(1)}, u32[]{:S(2)}, u32[]{:S(2)}) collective-permute-start(f32[2,2,16,1024]{3,2,1,0:T(8,128)S(1)} %maximum_select_fusion.5), channel_id=1, source_target_pairs={{0,64},{64,0},{32,96},{96,32},{128,192},{192,128},{160,224},{224,1... | collective-permute-start | bytes 786440 | tf_op jit(solution)/shard_map/ppermute | solution.py:19
  115.8 16.6 %collective-permute-start.14 = (f32[2,2,16,1024]{3,2,1,0:T(8,128)S(1)}, f32[2,2,16,1024]{3,2,1,0:T(8,128)S(1)}, u32[]{:S(2)}, u32[]{:S(2)}) collective-permute-start(f32[2,2,16,1024]{3,2,1,0:T(8,128)S(1)} %maximum_select_fusion.9), channel_id=1, source_target_pairs={{0,64},{64,0},{32,96},{96,32},{128,192},{192,128},{160,224},{224,1... | collective-permute-start | bytes 786440 | tf_op jit(solution)/shard_map/ppermute | solution.py:19
  121.3 14.1 %collective-permute-start.3 = (f32[2,2,16,1024]{3,2,1,0:T(8,128)S(1)}, f32[2,2,16,1024]{3,2,1,0:T(8,128)S(1)}, u32[]{:S(2)}, u32[]{:S(2)}) collective-permute-start(f32[2,2,16,1024]{3,2,1,0:T(8,128)S(1)} %maximum_select_fusion.2), channel_id=1, source_target_pairs={{0,32},{32,0},{64,96},{96,64},{128,160},{160,128},{192,224},{224,1... | collective-permute-start | bytes 786440 | tf_op jit(solution)/shard_map/ppermute | solution.py:19
  126.9 8.6 %collective-permute-start.7 = (f32[2,2,16,1024]{3,2,1,0:T(8,128)S(1)}, f32[2,2,16,1024]{3,2,1,0:T(8,128)S(1)}, u32[]{:S(2)}, u32[]{:S(2)}) collective-permute-start(f32[2,2,16,1024]{3,2,1,0:T(8,128)S(1)} %maximum_select_fusion.6), channel_id=1, source_target_pairs={{0,32},{32,0},{64,96},{96,64},{128,160},{160,128},{192,224},{224,1... | collective-permute-start | bytes 786440 | tf_op jit(solution)/shard_map/ppermute | solution.py:19
  132.5 3.5 collective-permute-start.15
  142.6 1.0 copy-start.1
  143.7 1.0 copy-start.3
  143.7 1.2 copy-start.5
  144.9 1.0 copy-start.28
  144.9 1.0 copy-start.29
  165.8 1.0 copy-start.2
  166.9 1.0 copy-start.4
  166.9 1.2 copy-start.6
  168.1 1.0 copy-start.26
  168.1 1.0 copy-start.27
  182.2 1.0 copy-start.8
  182.2 1.0 copy-start.33
  183.5 6.7 %collective-permute-start.20 = (f32[2,2,16,1024]{3,2,1,0:T(8,128)S(1)}, f32[2,2,16,1024]{3,2,1,0:T(8,128)S(1)}, u32[]{:S(2)}, u32[]{:S(2)}) collective-permute-start(f32[2,2,16,1024]{3,2,1,0:T(8,128)S(1)} %pad_maximum_fusion.5), channel_id=1, source_target_pairs={{0,32},{32,0},{64,96},{96,64},{128,160},{160,128},{192,224},{224,1... | collective-permute-start | bytes 786440 | tf_op jit(solution)/shard_map/ppermute | solution.py:19
  185.8 6.4 %collective-permute-start.8 = (f32[2,2,16,1024]{3,2,1,0:T(8,128)S(1)}, f32[2,2,16,1024]{3,2,1,0:T(8,128)S(1)}, u32[]{:S(2)}, u32[]{:S(2)}) collective-permute-start(f32[2,2,16,1024]{3,2,1,0:T(8,128)S(1)} %pad_maximum_fusion.2), channel_id=1, source_target_pairs={{0,32},{32,0},{64,96},{96,64},{128,160},{160,128},{192,224},{224,1... | collective-permute-start | bytes 786440 | tf_op jit(solution)/shard_map/ppermute | solution.py:19
  187.8 7.9 %collective-permute-start.16 = (f32[2,2,16,1024]{3,2,1,0:T(8,128)S(1)}, f32[2,2,16,1024]{3,2,1,0:T(8,128)S(1)}, u32[]{:S(2)}, u32[]{:S(2)}) collective-permute-start(f32[2,2,16,1024]{3,2,1,0:T(8,128)S(1)} %pad_maximum_fusion.4), channel_id=1, source_target_pairs={{0,32},{32,0},{64,96},{96,64},{128,160},{160,128},{192,224},{224,1... | collective-permute-start | bytes 786440 | tf_op jit(solution)/shard_map/ppermute | solution.py:19
  190.3 9.7 %collective-permute-start.21 = (f32[2,2,16,1024]{3,2,1,0:T(8,128)S(1)}, f32[2,2,16,1024]{3,2,1,0:T(8,128)S(1)}, u32[]{:S(2)}, u32[]{:S(2)}) collective-permute-start(f32[2,2,16,1024]{3,2,1,0:T(8,128)S(1)} %fusion.34), channel_id=1, source_target_pairs={{0,64},{64,0},{32,96},{96,32},{128,192},{192,128},{160,224},{224,1... | collective-permute-start | bytes 786440 | tf_op jit(solution)/shard_map/ppermute | solution.py:19
  192.3 13.2 %collective-permute-start.9 = (f32[2,2,16,1024]{3,2,1,0:T(8,128)S(1)}, f32[2,2,16,1024]{3,2,1,0:T(8,128)S(1)}, u32[]{:S(2)}, u32[]{:S(2)}) collective-permute-start(f32[2,2,16,1024]{3,2,1,0:T(8,128)S(1)} %fusion.26), channel_id=1, source_target_pairs={{0,64},{64,0},{32,96},{96,32},{128,192},{192,128},{160,224},{224,1... | collective-permute-start | bytes 786440 | tf_op jit(solution)/shard_map/ppermute | solution.py:19
  195.9 19.8 %collective-permute-start.17 = (f32[2,2,16,1024]{3,2,1,0:T(8,128)S(1)}, f32[2,2,16,1024]{3,2,1,0:T(8,128)S(1)}, u32[]{:S(2)}, u32[]{:S(2)}) collective-permute-start(f32[2,2,16,1024]{3,2,1,0:T(8,128)S(1)} %fusion.30), channel_id=1, source_target_pairs={{0,64},{64,0},{32,96},{96,32},{128,192},{192,128},{160,224},{224,1... | collective-permute-start | bytes 786440 | tf_op jit(solution)/shard_map/ppermute | solution.py:19
  200.1 19.1 %collective-permute-start.22 = (f32[2,2,16,1024]{3,2,1,0:T(8,128)S(1)}, f32[2,2,16,1024]{3,2,1,0:T(8,128)S(1)}, u32[]{:S(2)}, u32[]{:S(2)}) collective-permute-start(f32[2,2,16,1024]{3,2,1,0:T(8,128)S(1)} %fusion.35), channel_id=1, source_target_pairs={{0,128},{128,0},{32,160},{160,32},{64,192},{192,64},{96,224},{224,... | collective-permute-start | bytes 786440 | tf_op jit(solution)/shard_map/ppermute | solution.py:19
  205.7 32.6 %collective-permute-start.10 = (f32[2,2,16,1024]{3,2,1,0:T(8,128)S(1)}, f32[2,2,16,1024]{3,2,1,0:T(8,128)S(1)}, u32[]{:S(2)}, u32[]{:S(2)}) collective-permute-start(f32[2,2,16,1024]{3,2,1,0:T(8,128)S(1)} %fusion.27), channel_id=1, source_target_pairs={{0,128},{128,0},{32,160},{160,32},{64,192},{192,64},{96,224},{224,... | collective-permute-start | bytes 786440 | tf_op jit(solution)/shard_map/ppermute | solution.py:19
  215.9 37.0 %collective-permute-start.18 = (f32[2,2,16,1024]{3,2,1,0:T(8,128)S(1)}, f32[2,2,16,1024]{3,2,1,0:T(8,128)S(1)}, u32[]{:S(2)}, u32[]{:S(2)}) collective-permute-start(f32[2,2,16,1024]{3,2,1,0:T(8,128)S(1)} %fusion.31), channel_id=1, source_target_pairs={{0,128},{128,0},{32,160},{160,32},{64,192},{192,64},{96,224},{224,... | collective-permute-start | bytes 786440 | tf_op jit(solution)/shard_map/ppermute | solution.py:19
  219.3 35.7 %collective-permute-start.23 = (f32[2,2,16,1024]{3,2,1,0:T(8,128)S(1)}, f32[2,2,16,1024]{3,2,1,0:T(8,128)S(1)}, u32[]{:S(2)}, u32[]{:S(2)}) collective-permute-start(f32[2,2,16,1024]{3,2,1,0:T(8,128)S(1)} %fusion.36), channel_id=1, source_target_pairs={{0,256},{256,0},{32,288},{288,32},{64,320},{320,64},{96,352},{352,... | collective-permute-start | bytes 786440 | tf_op jit(solution)/shard_map/ppermute | solution.py:19
  238.4 52.4 %collective-permute-start.11 = (f32[2,2,16,1024]{3,2,1,0:T(8,128)S(1)}, f32[2,2,16,1024]{3,2,1,0:T(8,128)S(1)}, u32[]{:S(2)}, u32[]{:S(2)}) collective-permute-start(f32[2,2,16,1024]{3,2,1,0:T(8,128)S(1)} %fusion.28), channel_id=1, source_target_pairs={{0,256},{256,0},{32,288},{288,32},{64,320},{320,64},{96,352},{352,... | collective-permute-start | bytes 786440 | tf_op jit(solution)/shard_map/ppermute | solution.py:19
  253.0 37.8 %collective-permute-start.19 = (f32[2,2,16,1024]{3,2,1,0:T(8,128)S(1)}, f32[2,2,16,1024]{3,2,1,0:T(8,128)S(1)}, u32[]{:S(2)}, u32[]{:S(2)}) collective-permute-start(f32[2,2,16,1024]{3,2,1,0:T(8,128)S(1)} %fusion.32), channel_id=1, source_target_pairs={{0,256},{256,0},{32,288},{288,32},{64,320},{320,64},{96,352},{352,... | collective-permute-start | bytes 786440 | tf_op jit(solution)/shard_map/ppermute | solution.py:19
  255.1 33.9 %copy-start.35 = (f32[64,16]{0,1:T(8,128)S(1)}, f32[64,16]{0,1:T(8,128)}, u32[]{:S(2)}) copy-start(f32[64,16]{0,1:T(8,128)} %param.17) | copy-start | bytes 12292
  293.2 149.2 %copy-start.11 = (f32[64,1024]{1,0:T(8,128)S(1)}, f32[64,1024]{1,0:T(8,128)}, u32[]{:S(2)}) copy-start(f32[64,1024]{1,0:T(8,128)} %get-tuple-element.159) | copy-start | bytes 786436
  293.8 148.6 %copy-start.23 = (f32[64,64]{1,0:T(8,128)S(1)}, f32[64,64]{1,0:T(8,128)}, u32[]{:S(2)}) copy-start(f32[64,64]{1,0:T(8,128)} %param.16) | copy-start | bytes 49156
  442.5 3.0 copy-start.25
  (17 other events, 14.2 us)
Sparse Core Ops, SparseCore 0:
  290.9 151.4 all-reduce.5
where the time goes:
time: 513 us; the launch traced here: 505 us
  waiting for transfers between devices  243 us (47%)
  blocking collectives  111 us (22%)
  starting transfers between devices  59.6 us (12%)
  matrix products  33.2 us (6%)
  local copies, waits for them, and re-layouts  22.5 us (4%)
  other arithmetic  18.9 us (4%)
  between operations  16.9 us (3%)
    psum x1, waiting for transfers between devices, shards(): act_two_grad = lax.psum(act_two_part, 'chan')  148 us
    ppermute x24, waiting for transfers between devices, partner_2(): return lax.ppermute(block, axis, route)  95.2 us
    ppermute x24, starting transfers between devices, partner_2(): return lax.ppermute(block, axis, route)  59.5 us
    psum x1, blocking collectives, shards(): lax.psum((filter_part, matmul(act_one, pre_two_grad.T), matmul(position_t...  47.4 us
    psum x1, blocking collectives, shards(): lax.psum((jnp.sum(kernel_grad * kernel, axis=1), jnp.sum(through * produc...  33.7 us
    psum x1, blocking collectives, shards(): energy = lax.psum(jnp.sum(shaped * shaped, axis=1), 'ctx')  29.8 us
    dot_general x9, matrix products, matmul(): jnp.dot(left_side, right_side, precision=PRECISE, preferred_element_type=...  11.2 us
  transfers between devices with their start and end apart: 25, of which 16 were waited for; matrix products, arithmetic and copies ran while one was open for 2% of the time, Pallas kernels for 0%

commit v1 on v0

v1 whole, which is shorter than its diff:
```python
import functools
import math

import jax
import jax.numpy as jnp
import ml_dtypes
import numpy as np
from jax import lax
from jax.experimental import pallas as pl
from jax.experimental.pallas import tpu as pltpu
from jax.sharding import PartitionSpec as P

EPSILON = 1e-06
F32 = jnp.float32
BF16 = jnp.bfloat16
LANES = 128
X_CHIPS = 4
PI_HIGH = 3.140625
PI_MID = 9.67502593994140625e-4
PI_LOW = 1.509957990978376432e-7


def halves(table):
    high = table.astype(ml_dtypes.bfloat16)
    low = (table - high.astype(np.float64)).astype(ml_dtypes.bfloat16)
    return np.stack([high, low])


@functools.lru_cache(maxsize=None)
def tables(row_count):
    total = 2 * row_count * LANES
    ids = np.arange(row_count)
    lane_ids = np.arange(LANES)
    angle = 2 * np.pi * np.outer(ids + 0.5, ids) / (2 * row_count)
    first = np.concatenate([np.cos(angle), -np.sin(angle)], axis=0)
    last = first.T * (2.0 / total)
    lane_angle = 2 * np.pi * np.outer(lane_ids, lane_ids) / LANES
    cosine, sine = np.cos(lane_angle), np.sin(lane_angle)
    second = np.block([[cosine, -sine], [sine, cosine]])
    twist_angle = 2 * np.pi * np.outer(ids + 0.5, lane_ids) / total
    twist = np.stack([np.cos(twist_angle), np.sin(twist_angle)]).astype(np.float32)
    return halves(first), halves(last), halves(second), halves(second.T), twist


def exact_dot(left, right, left_dim, right_dim):
    return lax.dot_general(
        left,
        right,
        (((left_dim,), (right_dim,)), ((), ())),
        precision=lax.Precision.HIGHEST,
        preferred_element_type=F32,
    )


def split(value):
    high = value.astype(BF16)
    return high, (value - high.astype(F32)).astype(BF16)


def plain_dot(left, right):
    return jnp.dot(left, right, preferred_element_type=F32)


def table_left(table, value):
    high, low = split(value)
    return plain_dot(table[0], high) + (plain_dot(table[0], low) + plain_dot(table[1], high))


def table_right(value, table):
    high, low = split(value)
    return plain_dot(high, table[0]) + (plain_dot(low, table[0]) + plain_dot(high, table[1]))


def sine_cosine(angle):
    turns = jnp.floor(angle * (1.0 / math.pi) + 0.5)
    rest = ((angle - turns * PI_HIGH) - turns * PI_MID) - turns * PI_LOW
    odd = turns - 2.0 * jnp.floor(turns * 0.5)
    sign = 1.0 - 2.0 * odd
    square = rest * rest
    sine = 1.0 / math.factorial(13)
    for degree in (11, 9, 7, 5, 3, 1):
        sine = sine * square + (-1.0) ** (degree // 2) / math.factorial(degree)
    cosine = 1.0 / math.factorial(12)
    for degree in (10, 8, 6, 4, 2, 0):
        cosine = cosine * square + (-1.0) ** (degree // 2) / math.factorial(degree)
    return sine * (rest * sign), cosine * sign


def identity(size):
    rows = lax.broadcasted_iota(jnp.int32, (size, size), 0)
    cols = lax.broadcasted_iota(jnp.int32, (size, size), 1)
    return jnp.where(rows == cols, 1.0, 0.0).astype(F32)


def kernel(
    ctx_count,
    z_count,
    x_count,
    decay,
    skip,
    out_gate,
    in_gate,
    signal,
    grad_out,
    position_table,
    embed_weight,
    hidden_weight,
    filter_weight,
    first_table,
    last_table,
    second_table,
    back_table,
    twist,
    mixed,
    out_gate_grad,
    in_gate_grad,
    signal_grad,
    embed_grad,
    hidden_grad,
    filter_grad,
    skip_grad,
    position_grad,
    pair_send,
    pair_recv,
    raw_send,
    raw_recv,
    grad_send,
    grad_recv,
    inner_send,
    inner_recv,
    weight_all,
    weight_own,
    weight_turned,
    spread_send,
    spread_recv,
    part_send,
    part_recv,
    sum_send,
    sum_recv,
    total_recv,
    slab_send,
    slab_recv,
    place_send,
    place_recv,
    act_one_keep,
    act_two_keep,
    cos_one_keep,
    cos_two_keep,
    pair_sems,
    raw_sems,
    grad_sems,
    inner_sems,
    weight_sems,
    spread_sems,
    part_sems,
    sum_sems,
    total_sems,
    slab_sems,
    place_sems,
):
    chan_count = z_count * x_count
    rows = z_count
    channels = ctx_count
    hidden = hidden_weight.shape[0]
    features = position_table.shape[0]
    part_rows = hidden // z_count
    me = lax.axis_index("ctx")
    my_chan = lax.axis_index("chan")
    my_z = my_chan // x_count
    my_x = my_chan % x_count
    scale = (ctx_count * rows * LANES) ** (-0.5)

    def span(index, size):
        return pl.ds(pl.multiple_of(index * size, size), size)

    def ctx_copy(step, source, target, sems):
        peer = (me + step) % ctx_count
        return pltpu.make_async_remote_copy(
            src_ref=source(peer),
            dst_ref=target(me),
            send_sem=sems.at[0, step],
            recv_sem=sems.at[1, me],
            device_id={"ctx": peer},
            device_id_type=pl.DeviceIdType.MESH,
        )

    def ctx_arrival(step, source, target, sems):
        peer = (me + step) % ctx_count
        return pltpu.make_async_remote_copy(
            src_ref=source(peer),
            dst_ref=target(peer),
            send_sem=sems.at[0, step],
            recv_sem=sems.at[1, peer],
            device_id={"ctx": peer},
            device_id_type=pl.DeviceIdType.MESH,
        )

    def chan_copy(step, source, target, sems):
        peer = (my_chan + step) % chan_count
        return pltpu.make_async_remote_copy(
            src_ref=source(peer),
            dst_ref=target(my_chan),
            send_sem=sems.at[0, step],
            recv_sem=sems.at[1, my_chan],
            device_id={"chan": peer},
            device_id_type=pl.DeviceIdType.MESH,
        )

    def chan_arrival(step, source, target, sems):
        peer = (my_chan + step) % chan_count
        return pltpu.make_async_remote_copy(
            src_ref=source(peer),
            dst_ref=target(peer),
            send_sem=sems.at[0, step],
            recv_sem=sems.at[1, peer],
            device_id={"chan": peer},
            device_id_type=pl.DeviceIdType.MESH,
        )

    def z_copy(step, source, target, sems):
        peer = (my_z + step) % z_count
        return pltpu.make_async_remote_copy(
            src_ref=source(peer),
            dst_ref=target(my_z),
            send_sem=sems.at[0, step],
            recv_sem=sems.at[1, my_z],
            device_id={"chan": peer * x_count + my_x},
            device_id_type=pl.DeviceIdType.MESH,
        )

    def z_arrival(step, source, target, sems):
        peer = (my_z + step) % z_count
        return pltpu.make_async_remote_copy(
            src_ref=source(peer),
            dst_ref=target(peer),
            send_sem=sems.at[0, step],
            recv_sem=sems.at[1, peer],
            device_id={"chan": peer * x_count + my_x},
            device_id_type=pl.DeviceIdType.MESH,
        )

    def each(count, body):
        def one(step, carry):
            body(step)
            return carry

        lax.fori_loop(1, count, one, 0)

    pair_x = (ctx_copy, ctx_arrival, ctx_count,
              lambda p: pair_send.at[:, span(p, rows), :],
              lambda p: pair_recv.at[:, span(p, rows), :], pair_sems)
    raw_x = (ctx_copy, ctx_arrival, ctx_count,
             lambda p: raw_send.at[span(p, rows), :],
             lambda p: raw_recv.at[span(p, rows), :], raw_sems)
    grad_x = (ctx_copy, ctx_arrival, ctx_count,
              lambda p: grad_send.at[span(p, rows), :],
              lambda p: grad_recv.at[span(p, rows), :], grad_sems)
    inner_x = (ctx_copy, ctx_arrival, ctx_count,
               lambda p: inner_send.at[:, span(p, rows), :],
               lambda p: inner_recv.at[:, span(p, rows), :], inner_sems)
    weight_x = (chan_copy, chan_arrival, chan_count,
                lambda p: weight_own,
                lambda p: weight_all.at[span(p, channels), :], weight_sems)
    spread_x = (chan_copy, chan_arrival, chan_count,
                lambda p: spread_send.at[span(p // x_count, channels), :],
                lambda p: spread_recv.at[span(p, channels), :], spread_sems)
    slab_x = (ctx_copy, ctx_arrival, ctx_count,
              lambda p: slab_send, lambda p: slab_recv.at[p], slab_sems)
    part_x = (z_copy, z_arrival, z_count,
              lambda p: part_send.at[span(p, part_rows), :],
              lambda p: part_recv.at[p], part_sems)
    place_x = (z_copy, z_arrival, z_count,
               lambda p: place_send, lambda p: place_recv.at[p], place_sems)
    sum_x = (ctx_copy, ctx_arrival, ctx_count,
             lambda p: sum_send, lambda p: sum_recv.at[p], sum_sems)
    total_x = (z_copy, z_arrival, z_count,
               lambda p: total_recv.at[span(my_z, part_rows), :],
               lambda p: total_recv.at[span(p, part_rows), :], total_sems)

    def send(exchange):
        copy, _, count, source, target, sems = exchange
        each(count, lambda step: copy(step, source, target, sems).start())

    def arrive(exchange):
        _, arrival, count, source, target, sems = exchange
        each(count, lambda step: arrival(step, source, target, sems).wait_recv())

    def sent(exchange):
        copy, _, count, source, target, sems = exchange
        each(count, lambda step: copy(step, source, target, sems).wait_send())

    barrier = pltpu.get_barrier_semaphore()

    def greet_ctx(step):
        pl.semaphore_signal(
            barrier, inc=1, device_id={"ctx": (me + step) % ctx_count},
            device_id_type=pl.DeviceIdType.MESH,
        )

    def greet_chan(step):
        pl.semaphore_signal(
            barrier, inc=1, device_id={"chan": (my_chan + step) % chan_count},
            device_id_type=pl.DeviceIdType.MESH,
        )

    each(chan_count, greet_chan)
    each(ctx_count, greet_ctx)

    product = in_gate[...].astype(F32) * signal[...].astype(F32)
    through = grad_out[...].astype(F32) * out_gate[...].astype(F32)
    skip_part = jnp.sum(product * through, axis=1, keepdims=True)
    for row in range(rows):
        cut = slice(row * LANES, (row + 1) * LANES)
        pair_send[0, pl.ds(row, channels, stride=rows), :] = product[:, cut]
        pair_send[1, pl.ds(row, channels, stride=rows), :] = through[:, cut]
    weight_own[...] = jnp.zeros_like(weight_own)
    weight_own[:, 0:hidden] = exact_dot(identity(channels), filter_weight[...], 1, 1)

    pre_one = exact_dot(embed_weight[...], position_table[...], 0, 0)
    act_one, cos_one = sine_cosine(pre_one)
    act_one_keep[...] = act_one
    cos_one_keep[...] = cos_one
    pre_two = exact_dot(hidden_weight[...], act_one, 0, 0)
    act_two, cos_two = sine_cosine(pre_two)
    act_two_keep[...] = act_two
    cos_two_keep[...] = cos_two
    raw_filter = exact_dot(weight_own[:, 0:hidden], act_two, 1, 0)
    for row in range(rows):
        cut = slice(row * LANES, (row + 1) * LANES)
        raw_send[pl.ds(row, channels, stride=rows), :] = raw_filter[:, cut]

    pl.semaphore_wait(barrier, ctx_count + chan_count - 2)
    send(pair_x)
    send(raw_x)
    send(weight_x)
    pair_recv[:, span(me, rows), :] = pair_send[:, span(me, rows), :]
    raw_recv[span(me, rows), :] = raw_send[span(me, rows), :]
    weight_all[span(my_chan, channels), :] = weight_own[...]

    turn_cos = twist[0]
    turn_sin = twist[1]
    row_total = channels * rows

    def forward(field):
        half = table_left(first_table, field)
        real, imag = half[0:row_total], half[row_total:]
        turned = jnp.concatenate(
            [real * turn_cos + imag * turn_sin, imag * turn_cos - real * turn_sin], axis=1
        )
        whole = table_right(turned, second_table)
        return whole[:, 0:LANES], whole[:, LANES:]

    def times(first, second):
        real = first[0] * second[0] + first[1] * second[1]
        imag = first[0] * second[1] - first[1] * second[0]
        return jnp.concatenate([real, imag], axis=1)

    def inverse(spectrum):
        half = table_right(spectrum, back_table)
        real, imag = half[:, 0:LANES], half[:, LANES:]
        turned = jnp.concatenate(
            [real * turn_cos - imag * turn_sin, real * turn_sin + imag * turn_cos], axis=0
        )
        return table_left(last_table, turned)

    arrive(pair_x)
    own_product = pair_recv[0]
    own_through = pair_recv[1]
    product_spec = forward(own_product)
    through_spec = forward(own_through)
    kernel_grad = inverse(times(product_spec, through_spec))

    cells = (
        lax.broadcasted_iota(jnp.int32, (row_total, LANES), 0) * LANES
        + lax.broadcasted_iota(jnp.int32, (row_total, LANES), 1)
    ).astype(F32)
    envelope = jnp.exp(-decay[me] * cells)
    arrive(raw_x)
    shaped = raw_recv[...] * envelope
    energy = jnp.sum(jnp.sum(shaped * shaped, axis=0, keepdims=True), axis=1, keepdims=True)
    inverse_norm = lax.rsqrt(energy + EPSILON)
    filter_one = shaped * inverse_norm
    along = jnp.sum(jnp.sum(kernel_grad * filter_one, axis=0, keepdims=True), axis=1, keepdims=True)
    grad_send[...] = (kernel_grad - filter_one * along) * inverse_norm * envelope
    send(grad_x)
    grad_recv[span(me, rows), :] = grad_send[span(me, rows), :]

    filter_spec = forward(filter_one)
    conv = inverse(times((filter_spec[0], -filter_spec[1]), product_spec))
    inner_send[0] = conv + skip[me] * own_product
    back_conv = inverse(times(filter_spec, through_spec))
    inner_send[1] = back_conv + skip[me] * own_through
    send(inner_x)
    inner_recv[:, span(me, rows), :] = inner_send[:, span(me, rows), :]
    arrive(weight_x)
    weight_turned[...] = weight_all[...].T

    arrive(grad_x)
    blocks = []
    for row in range(rows):
        block = grad_recv[pl.ds(row, channels, stride=rows), :]
        spread_send[row * channels:(row + 1) * channels, :] = block
        blocks.append(block)
    send(spread_x)
    spread_recv[span(my_chan, channels), :] = spread_send[span(my_z, channels), :]
    slab_send[...] = jnp.broadcast_to(skip_part, (channels, LANES))
    slab_send[:, 0:hidden] = exact_dot(jnp.concatenate(blocks, axis=1), act_two_keep[...], 1, 1)
    send(slab_x)
    slab_recv[me] = slab_send[...]

    arrive(inner_x)
    for row in range(rows):
        cut = slice(row * LANES, (row + 1) * LANES)
        inner = inner_recv[0, pl.ds(row, channels, stride=rows), :]
        mixed[:, cut] = (out_gate[:, cut].astype(F32) * inner).astype(BF16)
        out_gate_grad[:, cut] = (grad_out[:, cut].astype(F32) * inner).astype(BF16)
        pull = inner_recv[1, pl.ds(row, channels, stride=rows), :]
        in_gate_grad[:, cut] = (pull * signal[:, cut].astype(F32)).astype(BF16)
        signal_grad[:, cut] = (pull * in_gate[:, cut].astype(F32)).astype(BF16)

    arrive(spread_x)
    mine = span(my_z, LANES)
    act_two_grad = exact_dot(weight_turned[0:hidden, :], spread_recv[...], 1, 0)
    pre_two_grad = act_two_grad * cos_two_keep[:, mine]
    act_one_grad = exact_dot(hidden_weight[...], pre_two_grad, 1, 0)
    pre_one_grad = act_one_grad * cos_one_keep[:, mine]
    part_send[...] = jnp.zeros_like(part_send)
    part_send[:, 0:hidden] = exact_dot(act_one_keep[:, mine], pre_two_grad, 1, 1)
    part_send[0:features, hidden:2 * hidden] = exact_dot(
        position_table[:, mine], pre_one_grad, 1, 1
    )
    send(part_x)
    part_recv[my_z] = part_send[span(my_z, part_rows), :]
    place_send[...] = jnp.zeros_like(place_send)
    place_send[0:features, :] = exact_dot(embed_weight[...], pre_one_grad, 1, 0)
    send(place_x)
    place_recv[my_z] = place_send[...]

    arrive(part_x)
    sum_send[...] = jnp.sum(part_recv[...], axis=0)
    send(sum_x)
    sum_recv[me] = sum_send[...]

    arrive(slab_x)
    slab = jnp.sum(slab_recv[...], axis=0) * scale
    filter_grad[...] = exact_dot(identity(hidden), slab[:, 0:hidden], 1, 1)
    picks = lax.broadcasted_iota(jnp.int32, (8, LANES), 1) == hidden
    skip_grad[...] = exact_dot(jnp.where(picks, 1.0, 0.0).astype(F32), slab, 1, 1)[0:1]
    arrive(place_x)
    for row in range(rows):
        position_grad[:, row * LANES:(row + 1) * LANES] = place_recv[row, 0:features, :]

    arrive(sum_x)
    total_recv[span(my_z, part_rows), :] = jnp.sum(sum_recv[...], axis=0) * scale
    send(total_x)
    for exchange in (pair_x, raw_x, weight_x, grad_x, inner_x, spread_x, slab_x, part_x, place_x, sum_x):
        sent(exchange)
    arrive(total_x)
    hidden_grad[...] = total_recv[:, 0:hidden]
    embed_grad[...] = total_recv[0:features, hidden:2 * hidden]
    sent(total_x)


def shards(
    x_count,
    out_gate,
    in_gate,
    signal,
    grad_out,
    position_table,
    embed_weight,
    hidden_weight,
    filter_weight,
    decay_rate,
    skip_gain,
):
    channels, length = signal.shape
    ctx_count = lax.axis_size("ctx")
    chan_count = lax.axis_size("chan")
    z_count = chan_count // x_count
    features, hidden = embed_weight.shape
    assert channels == ctx_count and length == z_count * LANES
    row_total = channels * z_count
    part_rows = hidden // z_count
    place_rows = (features + 7) // 8 * 8
    vmem = pl.BlockSpec(memory_space=pltpu.VMEM)
    smem = pl.BlockSpec(memory_space=pltpu.SMEM)
    block = jax.ShapeDtypeStruct((channels, length), BF16)
    scratch = [
        pltpu.VMEM((2, row_total, LANES), F32),
        pltpu.VMEM((2, row_total, LANES), F32),
        pltpu.VMEM((row_total, LANES), F32),
        pltpu.VMEM((row_total, LANES), F32),
        pltpu.VMEM((row_total, LANES), F32),
        pltpu.VMEM((row_total, LANES), F32),
        pltpu.VMEM((2, row_total, LANES), F32),
        pltpu.VMEM((2, row_total, LANES), F32),
        pltpu.VMEM((chan_count * channels, LANES), F32),
        pltpu.VMEM((channels, LANES), F32),
        pltpu.VMEM((LANES, chan_count * channels), F32),
        pltpu.VMEM((row_total, LANES), F32),
        pltpu.VMEM((chan_count * channels, LANES), F32),
        pltpu.VMEM((hidden, LANES), F32),
        pltpu.VMEM((z_count, part_rows, LANES), F32),
        pltpu.VMEM((part_rows, LANES), F32),
        pltpu.VMEM((ctx_count, part_rows, LANES), F32),
        pltpu.VMEM((hidden, LANES), F32),
        pltpu.VMEM((channels, LANES), F32),
        pltpu.VMEM((ctx_count, channels, LANES), F32),
        pltpu.VMEM((place_rows, LANES), F32),
        pltpu.VMEM((z_count, place_rows, LANES), F32),
        pltpu.VMEM((hidden, length), F32),
        pltpu.VMEM((hidden, length), F32),
        pltpu.VMEM((hidden, length), F32),
        pltpu.VMEM((hidden, length), F32),
    ]
    sem_counts = (
        [ctx_count] * 4 + [chan_count] * 2 + [z_count, ctx_count, z_count, ctx_count, z_count]
    )
    scratch += [pltpu.SemaphoreType.DMA((2, count)) for count in sem_counts]
    results = pl.pallas_call(
        functools.partial(kernel, ctx_count, z_count, x_count),
        out_shape=(
            block,
            block,
            block,
            block,
            jax.ShapeDtypeStruct((features, hidden), F32),
            jax.ShapeDtypeStruct((hidden, hidden), F32),
            jax.ShapeDtypeStruct((hidden, channels), F32),
            jax.ShapeDtypeStruct((1, channels), F32),
            jax.ShapeDtypeStruct((features, length), F32),
        ),
        in_specs=[smem] * 2 + [vmem] * 13,
        out_specs=tuple([vmem] * 9),
        scratch_shapes=scratch,
        compiler_params=pltpu.CompilerParams(
            collective_id=0, has_side_effects=True, vmem_limit_bytes=48 * 1024 * 1024
        ),
    )(
        decay_rate,
        skip_gain,
        out_gate,
        in_gate,
        signal,
        grad_out,
        position_table,
        embed_weight,
        hidden_weight,
        filter_weight,
        *(jnp.asarray(table) for table in tables(row_total)),
    )
    return results[:7] + (results[7].reshape(channels),) + results[8:]


def solution(mesh, x_count=X_CHIPS):
    placed = (
        P("chan", "ctx"),
        P("chan", "ctx"),
        P("chan", "ctx"),
        P("chan", "ctx"),
        P(None, "ctx"),
        P(),
        P(),
        P(None, "chan"),
        P("chan"),
        P("chan"),
    )
    return jax.shard_map(
        functools.partial(shards, x_count),
        mesh=mesh,
        in_specs=placed,
        out_specs=(
            P("chan", "ctx"),
            P("chan", "ctx"),
            P("chan", "ctx"),
            P("chan", "ctx"),
            P(),
            P(),
            P(None, "chan"),
            P("chan"),
            P(None, "ctx"),
        ),
        check_vma=False,
    )
```

time: 513 us -> 75.2 us (0.15); the launches traced: 505 us -> 74.5 us
  waiting for transfers between devices: 243 us -> 0 us
  blocking collectives: 111 us -> 0 us
  starting transfers between devices: 59.6 us -> 0 us
  Pallas kernels: 0 us -> 58.2 us
  matrix products: 33.2 us -> 0 us
  other arithmetic: 18.9 us -> 0 us
  between operations: 16.9 us -> 0.71 us
  local copies, waits for them, and re-layouts: 22.5 us -> 15.6 us
    psum x1 -> x0, waiting for transfers between devices: 148 us -> none  [shards(): act_two_grad = lax.psum(act_two_part, 'chan')]
    psum x3 -> x0, blocking collectives: 111 us -> none  [the longest x1 47.4 us: shards(): lax.psum((filter_part, matmul(act_one, pre_two_grad.T), matmul(position_t...]
    ppermute x24 -> x0, waiting for transfers between devices: 95.2 us -> none  [partner_2(): return lax.ppermute(block, axis, route)]
    ppermute x24 -> x0, starting transfers between devices: 59.5 us -> none  [partner_2(): return lax.ppermute(block, axis, route)]
    pallas_call x0 -> x1, Pallas kernels: none -> 58.2 us  [shards(): pl.pallas_call(functools.partial(kernel, ctx_count, z_count, x_count), ou...]
    dot_general x21 -> x0, matrix products: 33.2 us -> none  [the longest x9 11.2 us: matmul(): jnp.dot(left_side, right_side, precision=PRECISE, preferred_element_type=...]
    unnamed x80 -> x38, local copies, waits for them, and re-layouts: 5.39 us -> 15.6 us
    another operation x26 -> x0, local copies, waits for them, and re-layouts: 10.1 us -> none  [the longest x12 5.51 us: rotate_pair(): return jnp.stack([real_part, imag_part], axis=1)]
  transfers between devices with their start and end apart: 25 -> 0, of which waited for: 16 -> 0; matrix products, arithmetic and copies ran while one was open for 2% -> 0% of each run, Pallas kernels for 0% -> 0%
where the time goes in v1:
time: 75.2 us; the launch traced here: 74.5 us
  Pallas kernels  58.2 us (77%)
  local copies, waits for them, and re-layouts  15.6 us (21%)
    pallas_call x1, Pallas kernels, shards(): pl.pallas_call(functools.partial(kernel, ctx_count, z_count, x_count), ou...  58.2 us
    unnamed x38, local copies, waits for them, and re-layouts  15.6 us

profile of v1, /device:TPU:1, one launch (start us, length us, event | category | flops | bytes accessed | tf_op | source)
XLA Modules:
  0.0 74.5 jit_solution(4781396619265433470)
XLA Ops:
  0.6 0.0 copy-start.13
  0.7 0.0 copy-start.12
  0.7 0.0 copy-start.6
  0.7 0.8 %copy.24.filter_weight = f32[64,16]{1,0:T(8,128)S(1)} copy(f32[64,16]{0,1:T(8,128)} %param.22) | data formatting | bytes 8192 | tf_op args[7]
  1.5 0.0 copy-done.13
  1.5 0.0 copy-done.12
  1.5 0.0 copy-done.6
  1.5 0.0 copy-start
  1.5 0.9 %copy-done = bf16[2,256,256]{2,1,0:T(8,128)(2,1)S(1)} copy-done((bf16[2,256,256]{2,1,0:T(8,128)(2,1)S(1)}, bf16[2,256,256]{2,1,0:T(8,128)(2,1)}, u32[]{:S(2)}) %copy-start) | copy-done | bytes 262168
  2.4 0.0 copy-start.1
  2.4 0.9 %copy-done.1 = bf16[2,256,256]{2,1,0:T(8,128)(2,1)S(1)} copy-done((bf16[2,256,256]{2,1,0:T(8,128)(2,1)S(1)}, bf16[2,256,256]{2,1,0:T(8,128)(2,1)}, u32[]{:S(2)}) %copy-start.1) | copy-done | bytes 262168
  3.4 0.0 copy-start.2
  3.4 0.9 %copy-done.2 = f32[33,1024]{1,0:T(8,128)S(1)} copy-done((f32[33,1024]{1,0:T(8,128)S(1)}, f32[33,1024]{1,0:T(8,128)}, u32[]{:S(2)}) %copy-start.2) | copy-done | bytes 135192
  4.3 0.0 copy-start.3
  4.3 0.9 %copy-done.3 = f32[2,128,128]{2,1,0:T(8,128)S(1)} copy-done((f32[2,128,128]{2,1,0:T(8,128)S(1)}, f32[2,128,128]{2,1,0:T(8,128)}, u32[]{:S(2)}) %copy-start.3) | copy-done | bytes 131096
  5.2 0.0 copy-start.4
  5.2 0.9 %copy-done.4 = bf16[2,128,256]{2,1,0:T(8,128)(2,1)S(1)} copy-done((bf16[2,128,256]{2,1,0:T(8,128)(2,1)S(1)}, bf16[2,128,256]{2,1,0:T(8,128)(2,1)}, u32[]{:S(2)}) %copy-start.4) | copy-done | bytes 131096
  6.1 0.0 copy-start.5
  6.1 0.9 %copy-done.5 = bf16[2,256,128]{2,1,0:T(8,128)(2,1)S(1)} copy-done((bf16[2,256,128]{2,1,0:T(8,128)(2,1)S(1)}, bf16[2,256,128]{2,1,0:T(8,128)(2,1)}, u32[]{:S(2)}) %copy-start.5) | copy-done | bytes 131096
  7.0 0.0 copy-start.7
  7.0 0.8 %copy-done.7 = bf16[16,1024]{1,0:T(8,128)(2,1)S(1)} copy-done((bf16[16,1024]{1,0:T(8,128)(2,1)S(1)}, bf16[16,1024]{1,0:T(8,128)(2,1)}, u32[]{:S(2)}) %copy-start.7) | copy-done | bytes 32792
  7.8 0.0 copy-start.8
  7.8 0.8 %copy-done.8 = bf16[16,1024]{1,0:T(8,128)(2,1)S(1)} copy-done((bf16[16,1024]{1,0:T(8,128)(2,1)S(1)}, bf16[16,1024]{1,0:T(8,128)(2,1)}, u32[]{:S(2)}) %copy-start.8) | copy-done | bytes 32792
  8.5 0.0 copy-start.9
  8.5 0.8 %copy-done.9 = bf16[16,1024]{1,0:T(8,128)(2,1)S(1)} copy-done((bf16[16,1024]{1,0:T(8,128)(2,1)S(1)}, bf16[16,1024]{1,0:T(8,128)(2,1)}, u32[]{:S(2)}) %copy-start.9) | copy-done | bytes 32792
  9.3 0.0 copy-start.10
  9.3 0.8 %copy-done.10 = f32[64,64]{1,0:T(8,128)S(1)} copy-done((f32[64,64]{1,0:T(8,128)S(1)}, f32[64,64]{1,0:T(8,128)}, u32[]{:S(2)}) %copy-start.10) | copy-done | bytes 16408
  10.1 0.0 copy-start.11
  10.1 0.7 copy-done.11
  10.8 58.2 %shard_map.214 = (bf16[16,1024]{1,0:T(8,128)(2,1)S(1)}, bf16[16,1024]{1,0:T(8,128)(2,1)S(1)}, bf16[16,1024]{1,0:T(8,128)(2,1)S(1)}, bf16[16,1024]{1,0:T(8,128)(2...) custom-call(f32[16]{0:T(128)S(1)} %copy-done.12, ...), custom_call_target="tpu_custom_call" | custom-call | tf_op jit(solution)/shard_map/pallas_call | solution.py:521
  69.0 0.7 copy.25
  69.7 0.6 copy.34
  70.3 0.6 copy.35
  70.9 0.6 copy.36
  71.5 0.6 copy.37
  72.1 0.6 copy.38
  72.7 0.6 copy.39
  73.3 0.5 copy.40
  73.8 0.7 copy.41
Async XLA Ops:
  0.6 0.8 %copy-start.13 = (f32[16]{0:T(128)S(1)}, f32[16]{0:T(128)}, u32[]{:S(2)}) copy-start(f32[16]{0:T(128)} %skip.1) | copy-start | bytes 196
  0.7 0.8 %copy-start.12 = (f32[16]{0:T(128)S(1)}, f32[16]{0:T(128)}, u32[]{:S(2)}) copy-start(f32[16]{0:T(128)} %decay.1) | copy-start | bytes 196
  0.7 0.8 %copy-start.6 = (bf16[16,1024]{1,0:T(8,128)(2,1)S(1)}, bf16[16,1024]{1,0:T(8,128)(2,1)}, u32[]{:S(2)}) copy-start(bf16[16,1024]{1,0:T(8,128)(2,1)} %out_gate.1) | copy-start | bytes 98308
  1.5 1.0 %copy-start = (bf16[2,256,256]{2,1,0:T(8,128)(2,1)S(1)}, bf16[2,256,256]{2,1,0:T(8,128)(2,1)}, u32[]{:S(2)}) copy-start(bf16[2,256,256]{2,1,0:T(8,128)(2,1)} %constant.13.clone.back_table) | copy-start | bytes 786436
  2.4 0.9 %copy-start.1 = (bf16[2,256,256]{2,1,0:T(8,128)(2,1)S(1)}, bf16[2,256,256]{2,1,0:T(8,128)(2,1)}, u32[]{:S(2)}) copy-start(bf16[2,256,256]{2,1,0:T(8,128)(2,1)} %constant.12.clone.second_table) | copy-start | bytes 786436
  3.4 0.9 %copy-start.2 = (f32[33,1024]{1,0:T(8,128)S(1)}, f32[33,1024]{1,0:T(8,128)}, u32[]{:S(2)}) copy-start(f32[33,1024]{1,0:T(8,128)} %position_table.1) | copy-start | bytes 405508
  4.3 0.9 %copy-start.3 = (f32[2,128,128]{2,1,0:T(8,128)S(1)}, f32[2,128,128]{2,1,0:T(8,128)}, u32[]{:S(2)}) copy-start(f32[2,128,128]{2,1,0:T(8,128)} %constant.14.clone.twist) | copy-start | bytes 393220
  5.2 0.9 %copy-start.4 = (bf16[2,128,256]{2,1,0:T(8,128)(2,1)S(1)}, bf16[2,128,256]{2,1,0:T(8,128)(2,1)}, u32[]{:S(2)}) copy-start(bf16[2,128,256]{2,1,0:T(8,128)(2,1)} %constant.11.clone.last_table) | copy-start | bytes 393220
  6.1 0.9 %copy-start.5 = (bf16[2,256,128]{2,1,0:T(8,128)(2,1)S(1)}, bf16[2,256,128]{2,1,0:T(8,128)(2,1)}, u32[]{:S(2)}) copy-start(bf16[2,256,128]{2,1,0:T(8,128)(2,1)} %constant.10.clone.first_table) | copy-start | bytes 393220
  7.0 0.8 %copy-start.7 = (bf16[16,1024]{1,0:T(8,128)(2,1)S(1)}, bf16[16,1024]{1,0:T(8,128)(2,1)}, u32[]{:S(2)}) copy-start(bf16[16,1024]{1,0:T(8,128)(2,1)} %in_gate.1) | copy-start | bytes 98308
  7.8 0.8 %copy-start.8 = (bf16[16,1024]{1,0:T(8,128)(2,1)S(1)}, bf16[16,1024]{1,0:T(8,128)(2,1)}, u32[]{:S(2)}) copy-start(bf16[16,1024]{1,0:T(8,128)(2,1)} %signal.1) | copy-start | bytes 98308
  8.5 0.8 %copy-start.9 = (bf16[16,1024]{1,0:T(8,128)(2,1)S(1)}, bf16[16,1024]{1,0:T(8,128)(2,1)}, u32[]{:S(2)}) copy-start(bf16[16,1024]{1,0:T(8,128)(2,1)} %grad_out.1) | copy-start | bytes 98308
  9.3 0.8 %copy-start.10 = (f32[64,64]{1,0:T(8,128)S(1)}, f32[64,64]{1,0:T(8,128)}, u32[]{:S(2)}) copy-start(f32[64,64]{1,0:T(8,128)} %hidden_weight.1) | copy-start | bytes 49156
  10.1 0.7 copy-start.11

commit v2 on v1

v2 whole, which is shorter than its diff:
```python
import functools
import math

import jax
import jax.numpy as jnp
import ml_dtypes
import numpy as np
from jax import lax
from jax.experimental import pallas as pl
from jax.experimental.pallas import tpu as pltpu
from jax.sharding import PartitionSpec as P

EPSILON = 1e-06
F32 = jnp.float32
BF16 = jnp.bfloat16
LANES = 128
X_CHIPS = 4
INPUTS = 13
PI_HIGH = 3.140625
PI_MID = 9.67502593994140625e-4
PI_LOW = 1.509957990978376432e-7


def halves(table):
    high = table.astype(ml_dtypes.bfloat16)
    low = (table - high.astype(np.float64)).astype(ml_dtypes.bfloat16)
    return np.stack([high, low])


@functools.lru_cache(maxsize=None)
def tables(row_count):
    total = 2 * row_count * LANES
    ids = np.arange(row_count)
    lane_ids = np.arange(LANES)
    angle = 2 * np.pi * np.outer(ids + 0.5, ids) / (2 * row_count)
    first = np.concatenate([np.cos(angle), -np.sin(angle)], axis=0)
    last = first.T * (2.0 / total)
    lane_angle = 2 * np.pi * np.outer(lane_ids, lane_ids) / LANES
    cosine, sine = np.cos(lane_angle), np.sin(lane_angle)
    second = np.block([[cosine, -sine], [sine, cosine]])
    twist_angle = 2 * np.pi * np.outer(ids + 0.5, lane_ids) / total
    twist = np.stack([np.cos(twist_angle), np.sin(twist_angle)]).astype(np.float32)
    return halves(first), halves(last), halves(second), halves(second.T), twist


def exact_dot(left, right, left_dim, right_dim):
    return lax.dot_general(
        left,
        right,
        (((left_dim,), (right_dim,)), ((), ())),
        precision=lax.Precision.HIGHEST,
        preferred_element_type=F32,
    )


def split(value):
    high = value.astype(BF16)
    return high, (value - high.astype(F32)).astype(BF16)


def pair_dot(left, right, left_dim, right_dim):
    def one(first, second):
        return lax.dot_general(
            first, second, (((left_dim,), (right_dim,)), ((), ())), preferred_element_type=F32
        )

    return one(left[0], right[0]) + (one(left[0], right[1]) + one(left[1], right[0]))


def sine_cosine(angle):
    turns = jnp.floor(angle * (1.0 / math.pi) + 0.5)
    rest = ((angle - turns * PI_HIGH) - turns * PI_MID) - turns * PI_LOW
    odd = turns - 2.0 * jnp.floor(turns * 0.5)
    sign = 1.0 - 2.0 * odd
    square = rest * rest
    sine = 1.0 / math.factorial(13)
    for degree in (11, 9, 7, 5, 3, 1):
        sine = sine * square + (-1.0) ** (degree // 2) / math.factorial(degree)
    cosine = 1.0 / math.factorial(12)
    for degree in (10, 8, 6, 4, 2, 0):
        cosine = cosine * square + (-1.0) ** (degree // 2) / math.factorial(degree)
    return sine * (rest * sign), cosine * sign


def identity(size):
    rows = lax.broadcasted_iota(jnp.int32, (size, size), 0)
    cols = lax.broadcasted_iota(jnp.int32, (size, size), 1)
    return jnp.where(rows == cols, 1.0, 0.0).astype(F32)


def far_first(count):
    return sorted(range(1, count), key=lambda step: -min(step, count - step))


def kernel(ctx_count, z_count, x_count, decay, skip, *refs):
    sources, refs = refs[:INPUTS], refs[INPUTS:]
    (mixed, out_gate_grad, in_gate_grad, signal_grad, embed_grad, hidden_grad, filter_grad,
     skip_grad, position_grad), refs = refs[:9], refs[9:]
    locals_of, refs = refs[:INPUTS], refs[INPUTS:]
    (in_gate, signal, grad_out, out_gate, embed_weight, position_table, hidden_weight,
     filter_weight, first_ref, last_ref, second_ref, back_ref, twist) = locals_of
    (pair_send, pair_recv, raw_send, raw_recv, grad_send, grad_recv, inner_send, inner_recv,
     slab_send, slab_recv, part_send, part_recv, sum_send, sum_recv, total_recv,
     place_send, place_recv, place_sum, place_all), refs = refs[:19], refs[19:]
    (load_sems, pair_sems, raw_sems, grad_sems, inner_sems, slab_sems, part_sems, sum_sems,
     total_sems, place_sems, extra_sems, spread_sems, extra_spread_sems) = refs

    chan_count = z_count * x_count
    rows = z_count
    channels = ctx_count
    hidden = hidden_weight.shape[0]
    features = position_table.shape[0]
    part_rows = hidden // z_count
    me = lax.axis_index("ctx")
    my_chan = lax.axis_index("chan")
    my_z = my_chan // x_count
    my_x = my_chan % x_count
    scale = (ctx_count * rows * LANES) ** (-0.5)

    loads = {}
    for num, (source, local) in enumerate(zip(sources, locals_of)):
        loads[num] = pltpu.make_async_copy(source, local, load_sems.at[num])
        loads[num].start()

    def span(index, size):
        return pl.ds(pl.multiple_of(index * size, size), size)

    def ctx_peer(step):
        peer = (me + step) % ctx_count
        return peer, {"ctx": peer}

    def chan_peer(step):
        z_step, x_step = step // x_count, step % x_count
        peer = (my_z + z_step) % z_count * x_count + (my_x + x_step) % x_count
        return peer, {"chan": peer}

    def z_peer(step):
        peer = (my_z + step) % z_count
        return peer, {"chan": peer * x_count + my_x}

    def chan_far(step):
        z_step, x_step = step // x_count, step % x_count
        return -(min(z_step, z_count - z_step) + min(x_step, x_count - x_step))

    ctx_steps = far_first(ctx_count)
    z_steps = far_first(z_count)
    chan_steps = sorted(range(1, chan_count), key=chan_far)
    over_ctx = (ctx_peer, me, ctx_steps)
    over_chan = (chan_peer, my_chan, chan_steps)
    over_z = (z_peer, my_z, z_steps)

    def copy_of(exchange, step, slot):
        (peer_of, own, _), source, target, sems = exchange
        peer, device = peer_of(step)
        slot_index = own if slot == "own" else peer
        return pltpu.make_async_remote_copy(
            src_ref=source(peer),
            dst_ref=target(slot_index),
            send_sem=sems.at[0, step],
            recv_sem=sems.at[1, slot_index],
            device_id=device,
            device_id_type=pl.DeviceIdType.MESH,
        )

    def send(exchange):
        for step in exchange[0][2]:
            copy_of(exchange, step, "own").start()

    def arrive(exchange):
        for step in reversed(exchange[0][2]):
            copy_of(exchange, step, "peer").wait_recv()

    def sent(exchange):
        for step in exchange[0][2]:
            copy_of(exchange, step, "own").wait_send()

    pair_x = (over_ctx, lambda p: pair_send.at[:, span(p, rows), :],
              lambda p: pair_recv.at[:, span(p, rows), :], pair_sems)
    raw_x = (over_ctx, lambda p: raw_send.at[span(p, rows), :],
             lambda p: raw_recv.at[span(p, rows), :], raw_sems)
    grad_x = (over_ctx, lambda p: grad_send.at[span(p, rows), :],
              lambda p: grad_recv.at[span(p, rows), :], grad_sems)
    inner_x = (over_ctx, lambda p: inner_send.at[:, span(p, rows), :],
               lambda p: inner_recv.at[:, span(p, rows), :], inner_sems)
    slab_x = (over_ctx, lambda p: slab_send, lambda p: slab_recv.at[p], slab_sems)
    part_x = (over_chan, lambda p: part_send.at[span(p // x_count, part_rows), :],
              lambda p: part_recv.at[p], part_sems)
    sum_x = (over_ctx, lambda p: sum_send, lambda p: sum_recv.at[p], sum_sems)
    total_x = (over_z, lambda p: total_recv.at[span(my_z, part_rows), :],
               lambda p: total_recv.at[span(p, part_rows), :], total_sems)
    place_x = (over_chan, lambda p: place_send.at[span(p, rows), :], lambda p: place_recv.at[0, p], place_sems)
    spread_x = (over_chan, lambda p: place_sum.at[0],
                lambda p: place_all.at[span(p, rows), :], spread_sems)
    extras = range(chan_count, features)

    def extra_x(num):
        return (over_chan, lambda p: place_send.at[pl.ds(num * rows, rows), :],
                lambda p: place_recv.at[1 + num - chan_count, p],
                extra_sems.at[num - chan_count])

    def extra_spread_x(num):
        return (over_chan, lambda p: place_sum.at[1 + num - chan_count],
                lambda p: place_all.at[pl.ds(num * rows, rows), :],
                extra_spread_sems.at[num - chan_count])

    barrier = pltpu.get_barrier_semaphore()
    for step in chan_steps:
        pl.semaphore_signal(barrier, inc=1, device_id=chan_peer(step)[1],
                            device_id_type=pl.DeviceIdType.MESH)
    for step in ctx_steps:
        pl.semaphore_signal(barrier, inc=1, device_id=ctx_peer(step)[1],
                            device_id_type=pl.DeviceIdType.MESH)

    for num in range(4):
        loads[num].wait()
    product = in_gate[...].astype(F32) * signal[...].astype(F32)
    through = grad_out[...].astype(F32) * out_gate[...].astype(F32)
    skip_part = jnp.sum(product * through, axis=1, keepdims=True)
    for row in range(rows):
        cut = slice(row * LANES, (row + 1) * LANES)
        pair_send[0, pl.ds(row, channels, stride=rows), :] = product[:, cut]
        pair_send[1, pl.ds(row, channels, stride=rows), :] = through[:, cut]

    for num in range(4, 8):
        loads[num].wait()
    pre_one = exact_dot(embed_weight[...], position_table[...], 0, 0)
    act_one, cos_one = sine_cosine(pre_one)
    pre_two = exact_dot(hidden_weight[...], act_one, 0, 0)
    act_two, cos_two = sine_cosine(pre_two)
    act_two_halves = split(act_two)
    filter_halves = split(filter_weight[...])
    raw_filter = pair_dot(filter_halves, act_two_halves, 1, 0)
    for row in range(rows):
        cut = slice(row * LANES, (row + 1) * LANES)
        raw_send[pl.ds(row, channels, stride=rows), :] = raw_filter[:, cut]

    pl.semaphore_wait(barrier, ctx_count + chan_count - 2)
    send(pair_x)
    send(raw_x)
    pair_recv[:, span(me, rows), :] = pair_send[:, span(me, rows), :]
    raw_recv[span(me, rows), :] = raw_send[span(me, rows), :]
    for num in range(8, INPUTS):
        loads[num].wait()

    turn_cos = twist[0]
    turn_sin = twist[1]
    row_total = channels * rows

    def both(table):
        return table[0], table[1]

    def forward(fields):
        half = pair_dot(both(first_ref), split(jnp.concatenate(fields, axis=1)), 1, 0)
        turned = []
        for num in range(len(fields)):
            cut = slice(num * LANES, (num + 1) * LANES)
            real, imag = half[0:row_total, cut], half[row_total:, cut]
            turned.append(jnp.concatenate(
                [real * turn_cos + imag * turn_sin, imag * turn_cos - real * turn_sin], axis=1
            ))
        whole = pair_dot(split(jnp.concatenate(turned, axis=0)), both(second_ref), 1, 0)
        return [(whole[num * row_total:(num + 1) * row_total, 0:LANES],
                 whole[num * row_total:(num + 1) * row_total, LANES:]) for num in range(len(fields))]

    def times(first, second):
        real = first[0] * second[0] + first[1] * second[1]
        imag = first[0] * second[1] - first[1] * second[0]
        return jnp.concatenate([real, imag], axis=1)

    def inverse(spectra):
        half = pair_dot(split(jnp.concatenate(spectra, axis=0)), both(back_ref), 1, 0)
        turned = []
        for num in range(len(spectra)):
            cut = slice(num * row_total, (num + 1) * row_total)
            real, imag = half[cut, 0:LANES], half[cut, LANES:]
            turned.append(jnp.concatenate(
                [real * turn_cos - imag * turn_sin, real * turn_sin + imag * turn_cos], axis=0
            ))
        return pair_dot(both(last_ref), split(jnp.concatenate(turned, axis=1)), 1, 0)

    cells = (
        lax.broadcasted_iota(jnp.int32, (row_total, LANES), 0) * LANES
        + lax.broadcasted_iota(jnp.int32, (row_total, LANES), 1)
    ).astype(F32)
    envelope = jnp.exp(-decay[me] * cells)

    arrive(pair_x)
    own_product = pair_recv[0]
    own_through = pair_recv[1]
    product_spec, through_spec = forward([own_product, own_through])
    kernel_grad = inverse([times(product_spec, through_spec)])

    arrive(raw_x)
    shaped = raw_recv[...] * envelope
    energy = jnp.sum(jnp.sum(shaped * shaped, axis=0, keepdims=True), axis=1, keepdims=True)
    inverse_norm = lax.rsqrt(energy + EPSILON)
    filter_one = shaped * inverse_norm
    along = jnp.sum(jnp.sum(kernel_grad * filter_one, axis=0, keepdims=True), axis=1, keepdims=True)
    grad_send[...] = (kernel_grad - filter_one * along) * inverse_norm * envelope
    send(grad_x)
    grad_recv[span(me, rows), :] = grad_send[span(me, rows), :]

    (filter_spec,) = forward([filter_one])
    convs = inverse([
        times((filter_spec[0], -filter_spec[1]), product_spec), times(filter_spec, through_spec)
    ])
    inner_send[0] = convs[:, 0:LANES] + skip[me] * own_product
    inner_send[1] = convs[:, LANES:] + skip[me] * own_through
    send(inner_x)
    inner_recv[:, span(me, rows), :] = inner_send[:, span(me, rows), :]

    arrive(grad_x)
    raw_grad = jnp.concatenate(
        [grad_recv[pl.ds(row, channels, stride=rows), :] for row in range(rows)], axis=1
    )
    raw_grad_halves = split(raw_grad)
    pre_two_grad = pair_dot(filter_halves, raw_grad_halves, 0, 0) * cos_two
    pre_two_halves = split(pre_two_grad)
    pre_one_grad = pair_dot(split(hidden_weight[...]), pre_two_halves, 1, 0) * cos_one
    pre_one_halves = split(pre_one_grad)
    part_send[...] = jnp.zeros_like(part_send)
    part_send[:, 0:hidden] = pair_dot(split(act_one), pre_two_halves, 1, 1)
    part_send[0:features, hidden:2 * hidden] = pair_dot(
        split(position_table[...]), pre_one_halves, 1, 1
    )
    send(part_x)
    part_recv[my_chan] = part_send[span(my_z, part_rows), :]
    place = pair_dot(split(embed_weight[...]), pre_one_halves, 1, 0)
    for row in range(rows):
        place_send[pl.ds(row, features, stride=rows), :] = place[:, row * LANES:(row + 1) * LANES]
    send(place_x)
    place_recv[0, my_chan] = place_send[span(my_chan, rows), :]
    for num in extras:
        for step in chan_steps:
            peer = chan_peer(step)[0]

            @pl.when(peer == 0)
            def _():
                copy_of(extra_x(num), step, "own").start()

        place_recv[1 + num - chan_count, my_chan] = place_send[num * rows:(num + 1) * rows, :]
    slab_send[...] = jnp.broadcast_to(skip_part, (channels, LANES))
    slab_send[:, 0:hidden] = pair_dot(raw_grad_halves, act_two_halves, 1, 1)
    send(slab_x)
    slab_recv[me] = slab_send[...]

    arrive(inner_x)
    for row in range(rows):
        cut = slice(row * LANES, (row + 1) * LANES)
        inner = inner_recv[0, pl.ds(row, channels, stride=rows), :]
        mixed[:, cut] = (out_gate[:, cut].astype(F32) * inner).astype(BF16)
        out_gate_grad[:, cut] = (grad_out[:, cut].astype(F32) * inner).astype(BF16)
        pull = inner_recv[1, pl.ds(row, channels, stride=rows), :]
        in_gate_grad[:, cut] = (pull * signal[:, cut].astype(F32)).astype(BF16)
        signal_grad[:, cut] = (pull * in_gate[:, cut].astype(F32)).astype(BF16)

    arrive(part_x)
    sum_send[...] = jnp.sum(part_recv[...], axis=0)
    send(sum_x)
    sum_recv[me] = sum_send[...]

    arrive(place_x)
    place_sum[0] = jnp.sum(place_recv[0], axis=0)
    send(spread_x)
    place_all[span(my_chan, rows), :] = place_sum[0]
    for num in extras:

        @pl.when(my_chan == 0)
        def _():
            arrive(extra_x(num))
            place_sum[1 + num - chan_count] = jnp.sum(place_recv[1 + num - chan_count], axis=0)
            send(extra_spread_x(num))
            place_all[num * rows:(num + 1) * rows, :] = place_sum[1 + num - chan_count]

    arrive(slab_x)
    slab = jnp.sum(slab_recv[...], axis=0) * scale
    filter_grad[...] = slab[:, 0:hidden]
    picks = lax.broadcasted_iota(jnp.int32, (8, LANES), 1) == hidden
    skip_grad[...] = exact_dot(jnp.where(picks, 1.0, 0.0).astype(F32), slab, 1, 1)[0:1]

    arrive(sum_x)
    total_recv[span(my_z, part_rows), :] = jnp.sum(sum_recv[...], axis=0) * scale
    send(total_x)
    for exchange in (pair_x, raw_x, grad_x, inner_x, slab_x, part_x, sum_x, place_x):
        sent(exchange)

    arrive(spread_x)
    for num in extras:

        @pl.when(my_chan == 0)
        def _():
            sent(extra_spread_x(num))

        @pl.when(my_chan != 0)
        def _():
            for step in chan_steps:

                @pl.when(chan_peer(step)[0] == 0)
                def _():
                    copy_of(extra_x(num), step, "own").wait_send()
                    copy_of(extra_spread_x(num), step, "first").wait_recv()

    for row in range(rows):
        position_grad[:, row * LANES:(row + 1) * LANES] = place_all[
            pl.ds(row, features, stride=rows), :
        ]
    sent(spread_x)
    arrive(total_x)
    hidden_grad[...] = total_recv[:, 0:hidden]
    embed_grad[...] = total_recv[0:features, hidden:2 * hidden]
    sent(total_x)


def put_out(*refs):
    count = len(refs) // 2
    copies = [
        pltpu.make_async_copy(refs[num], refs[count + num], refs[-1].at[num]) for num in range(count)
    ]
    for copy in copies:
        copy.start()
    for copy in copies:
        copy.wait()


def shards(
    x_count,
    out_gate,
    in_gate,
    signal,
    grad_out,
    position_table,
    embed_weight,
    hidden_weight,
    filter_weight,
    decay_rate,
    skip_gain,
):
    channels, length = signal.shape
    ctx_count = lax.axis_size("ctx")
    chan_count = lax.axis_size("chan")
    z_count = chan_count // x_count
    features, hidden = embed_weight.shape
    assert channels == ctx_count and length == z_count * LANES
    row_total = channels * z_count
    part_rows = hidden // z_count
    extra_count = max(1, features - chan_count)
    vmem = pl.BlockSpec(memory_space=pltpu.VMEM)
    smem = pl.BlockSpec(memory_space=pltpu.SMEM)
    hbm = pl.BlockSpec(memory_space=pltpu.HBM)
    operands = (
        in_gate,
        signal,
        grad_out,
        out_gate,
        embed_weight,
        position_table,
        hidden_weight,
        filter_weight.T,
        *(jnp.asarray(table) for table in tables(row_total)),
    )
    block = jax.ShapeDtypeStruct((channels, length), BF16)
    shapes = (
        block,
        block,
        block,
        block,
        jax.ShapeDtypeStruct((features, hidden), F32),
        jax.ShapeDtypeStruct((hidden, hidden), F32),
        jax.ShapeDtypeStruct((channels, hidden), F32),
        jax.ShapeDtypeStruct((1, channels), F32),
        jax.ShapeDtypeStruct((features, length), F32),
    )
    scratch = [pltpu.VMEM(operand.shape, operand.dtype) for operand in operands]
    scratch += [
        pltpu.VMEM(shape, F32)
        for shape in (
            (2, row_total, LANES),
            (2, row_total, LANES),
            (row_total, LANES),
            (row_total, LANES),
            (row_total, LANES),
            (row_total, LANES),
            (2, row_total, LANES),
            (2, row_total, LANES),
            (channels, LANES),
            (ctx_count, channels, LANES),
            (hidden, LANES),
            (chan_count, part_rows, LANES),
            (part_rows, LANES),
            (ctx_count, part_rows, LANES),
            (hidden, LANES),
            (features * z_count, LANES),
            (1 + extra_count, chan_count, z_count, LANES),
            (1 + extra_count, z_count, LANES),
            (features * z_count, LANES),
        )
    ]
    scratch += [pltpu.SemaphoreType.DMA((INPUTS,))]
    scratch += [
        pltpu.SemaphoreType.DMA((2, count))
        for count in [ctx_count] * 5 + [chan_count, ctx_count, z_count, chan_count]
    ]
    scratch += [
        pltpu.SemaphoreType.DMA((extra_count, 2, chan_count)),
        pltpu.SemaphoreType.DMA((2, chan_count)),
        pltpu.SemaphoreType.DMA((extra_count, 2, chan_count)),
    ]
    results = pl.pallas_call(
        functools.partial(kernel, ctx_count, z_count, x_count),
        out_shape=shapes,
        in_specs=[smem] * 2 + [hbm] * INPUTS,
        out_specs=tuple([vmem] * 9),
        scratch_shapes=scratch,
        compiler_params=pltpu.CompilerParams(
            collective_id=0, has_side_effects=True, vmem_limit_bytes=67043328
        ),
    )(decay_rate, skip_gain, *operands)
    results = pl.pallas_call(
        put_out,
        out_shape=shapes,
        in_specs=[vmem] * 9,
        out_specs=tuple([hbm] * 9),
        scratch_shapes=[pltpu.SemaphoreType.DMA((9,))],
    )(*results)
    results = list(results)
    results[6] = results[6].T
    results[7] = results[7].reshape(channels)
    return tuple(results)


def solution(mesh, x_count=X_CHIPS):
    placed = (
        P("chan", "ctx"),
        P("chan", "ctx"),
        P("chan", "ctx"),
        P("chan", "ctx"),
        P(None, "ctx"),
        P(),
        P(),
        P(None, "chan"),
        P("chan"),
        P("chan"),
    )
    return jax.shard_map(
        functools.partial(shards, x_count),
        mesh=mesh,
        in_specs=placed,
        out_specs=(
            P("chan", "ctx"),
            P("chan", "ctx"),
            P("chan", "ctx"),
            P("chan", "ctx"),
            P(),
            P(),
            P(None, "chan"),
            P("chan"),
            P(None, "ctx"),
        ),
        check_vma=False,
    )
```

time: 75.2 us -> 54 us (0.72)
  local copies, waits for them, and re-layouts: 15.6 us -> 0 us
  Pallas kernels: 58.2 us -> 53.2 us
    unnamed x38 -> x0, local copies, waits for them, and re-layouts: 15.6 us -> none
    pallas_call x1, Pallas kernels: 58.2 us -> 51.3 us  [shards(): pl.pallas_call(functools.partial(kernel, ctx_count, z_count, x_count), ou...]
    pallas_call x0 -> x1, Pallas kernels: none -> 1.87 us  [shards(): pl.pallas_call(put_out, out_shape=shapes, in_specs=[vmem] * 9, out_specs=...]
where the time goes in v2:
time: 54 us; the launch traced here: 53.9 us
  Pallas kernels  53.2 us (99%)
  between operations  0.65 us (1%)
    pallas_call x1, Pallas kernels, shards(): pl.pallas_call(functools.partial(kernel, ctx_count, z_count, x_count), ou...  51.3 us
    pallas_call x1, Pallas kernels, shards(): pl.pallas_call(put_out, out_shape=shapes, in_specs=[vmem] * 9, out_specs=...  1.87 us

profile of v2, /device:TPU:1, one launch (start us, length us, event | category | flops | bytes accessed | tf_op | source)
XLA Modules:
  0.0 53.9 jit_solution(5240239919894450241)
XLA Ops:
  0.6 51.3 %shard_map.214 = (bf16[16,1024]{1,0:T(8,128)(2,1)}, bf16[16,1024]{1,0:T(8,128)(2,1)}, bf16[16,1024]{1,0:T(8,128)(2,1)}, bf16[16,1024]{1,0:T(8,128)(2,1)}, f32[33...) custom-call(f32[16]{0:T(128)} %decay.1, f32[16]{0:T(128)} %skip.1, ...), custom_call_target="tpu_custom_call" | custom-call | tf_op jit(solution)/shard_map/pallas_call | solution.py:508
  52.0 1.9 %shard_map.215 = (bf16[16,1024]{1,0:T(8,128)(2,1)}, bf16[16,1024]{1,0:T(8,128)(2,1)}, bf16[16,1024]{1,0:T(8,128)(2,1)}, bf16[16,1024]{1,0:T(8,128)(2,1)}, f32[33...) custom-call(bf16[16,1024]{1,0:T(8,128)(2,1)} %get-tuple-element.27.refs_0_, ...), custom_call_target="tpu_custom_call" | custom-call | tf_op jit(solution)/shard_map/pallas_call | solution.py:518

commit v3 on v2

--- a/solution.py
+++ b/solution.py
@@ -15,7 +15,7 @@
 BF16 = jnp.bfloat16
 LANES = 128
 X_CHIPS = 4
-INPUTS = 13
+INPUTS = 15
 PI_HIGH = 3.140625
 PI_MID = 9.67502593994140625e-4
 PI_LOW = 1.509957990978376432e-7
@@ -92,18 +92,18 @@
     return sorted(range(1, count), key=lambda step: -min(step, count - step))
 
 
-def kernel(ctx_count, z_count, x_count, decay, skip, *refs):
+def kernel(ctx_count, z_count, x_count, *refs):
     sources, refs = refs[:INPUTS], refs[INPUTS:]
     (mixed, out_gate_grad, in_gate_grad, signal_grad, embed_grad, hidden_grad, filter_grad,
      skip_grad, position_grad), refs = refs[:9], refs[9:]
     locals_of, refs = refs[:INPUTS], refs[INPUTS:]
     (in_gate, signal, grad_out, out_gate, embed_weight, position_table, hidden_weight,
-     filter_weight, first_ref, last_ref, second_ref, back_ref, twist) = locals_of
+     filter_weight, decay, skip, first_ref, last_ref, second_ref, back_ref, twist) = locals_of
     (pair_send, pair_recv, raw_send, raw_recv, grad_send, grad_recv, inner_send, inner_recv,
      slab_send, slab_recv, part_send, part_recv, sum_send, sum_recv, total_recv,
      place_send, place_recv, place_sum, place_all), refs = refs[:19], refs[19:]
     (load_sems, pair_sems, raw_sems, grad_sems, inner_sems, slab_sems, part_sems, sum_sems,
-     total_sems, place_sems, extra_sems, spread_sems, extra_spread_sems) = refs
+     total_sems, place_sems, spread_sems) = refs
 
     chan_count = z_count * x_count
     rows = z_count
@@ -125,17 +125,21 @@
     def span(index, size):
         return pl.ds(pl.multiple_of(index * size, size), size)
 
+    def ahead(index, step, count):
+        index = index + step
+        return jnp.where(index >= count, index - count, index) if step else index
+
     def ctx_peer(step):
-        peer = (me + step) % ctx_count
+        peer = ahead(me, step, ctx_count)
         return peer, {"ctx": peer}
 
     def chan_peer(step):
         z_step, x_step = step // x_count, step % x_count
-        peer = (my_z + z_step) % z_count * x_count + (my_x + x_step) % x_count
+        peer = ahead(my_z, z_step, z_count) * x_count + ahead(my_x, x_step, x_count)
         return peer, {"chan": peer}
 
     def z_peer(step):
-        peer = (my_z + step) % z_count
+        peer = ahead(my_z, step, z_count)
         return peer, {"chan": peer * x_count + my_x}
 
     def chan_far(step):
@@ -188,20 +192,11 @@
     sum_x = (over_ctx, lambda p: sum_send, lambda p: sum_recv.at[p], sum_sems)
     total_x = (over_z, lambda p: total_recv.at[span(my_z, part_rows), :],
                lambda p: total_recv.at[span(p, part_rows), :], total_sems)
-    place_x = (over_chan, lambda p: place_send.at[span(p, rows), :], lambda p: place_recv.at[0, p], place_sems)
-    spread_x = (over_chan, lambda p: place_sum.at[0],
+    place_x = (over_chan, lambda p: place_send.at[span(p, rows), :], lambda p: place_recv.at[p], place_sems)
+    spread_x = (over_chan, lambda p: place_sum,
                 lambda p: place_all.at[span(p, rows), :], spread_sems)
-    extras = range(chan_count, features)
-
-    def extra_x(num):
-        return (over_chan, lambda p: place_send.at[pl.ds(num * rows, rows), :],
-                lambda p: place_recv.at[1 + num - chan_count, p],
-                extra_sems.at[num - chan_count])
-
-    def extra_spread_x(num):
-        return (over_chan, lambda p: place_sum.at[1 + num - chan_count],
-                lambda p: place_all.at[pl.ds(num * rows, rows), :],
-                extra_spread_sems.at[num - chan_count])
+    corner = (features + 7) // 8 * 8
+    corner_rows = rows * LANES // hidden
 
     barrier = pltpu.get_barrier_semaphore()
     for step in chan_steps:
@@ -221,7 +216,7 @@
         pair_send[0, pl.ds(row, channels, stride=rows), :] = product[:, cut]
         pair_send[1, pl.ds(row, channels, stride=rows), :] = through[:, cut]
 
-    for num in range(4, 8):
+    for num in range(4, 10):
         loads[num].wait()
     pre_one = exact_dot(embed_weight[...], position_table[...], 0, 0)
     act_one, cos_one = sine_cosine(pre_one)
@@ -239,7 +234,7 @@
     send(raw_x)
     pair_recv[:, span(me, rows), :] = pair_send[:, span(me, rows), :]
     raw_recv[span(me, rows), :] = raw_send[span(me, rows), :]
-    for num in range(8, INPUTS):
+    for num in range(10, INPUTS):
         loads[num].wait()
 
     turn_cos = twist[0]
@@ -323,26 +318,23 @@
     part_send[0:features, hidden:2 * hidden] = pair_dot(
         split(position_table[...]), pre_one_halves, 1, 1
     )
+    place = pair_dot(split(embed_weight[...]), pre_one_halves, 1, 0)
+    for num in range(corner_rows):
+        part_send[corner + num:corner + num + 1, hidden:2 * hidden] = place[
+            chan_count:features, num * hidden:(num + 1) * hidden
+        ]
     send(part_x)
     part_recv[my_chan] = part_send[span(my_z, part_rows), :]
-    place = pair_dot(split(embed_weight[...]), pre_one_halves, 1, 0)
-    for row in range(rows):
-        place_send[pl.ds(row, features, stride=rows), :] = place[:, row * LANES:(row + 1) * LANES]
-    send(place_x)
-    place_recv[0, my_chan] = place_send[span(my_chan, rows), :]
-    for num in extras:
-        for step in chan_steps:
-            peer = chan_peer(step)[0]
-
-            @pl.when(peer == 0)
-            def _():
-                copy_of(extra_x(num), step, "own").start()
-
-        place_recv[1 + num - chan_count, my_chan] = place_send[num * rows:(num + 1) * rows, :]
     slab_send[...] = jnp.broadcast_to(skip_part, (channels, LANES))
     slab_send[:, 0:hidden] = pair_dot(raw_grad_halves, act_two_halves, 1, 1)
     send(slab_x)
     slab_recv[me] = slab_send[...]
+    for row in range(rows):
+        place_send[pl.ds(row, chan_count, stride=rows), :] = place[
+            0:chan_count, row * LANES:(row + 1) * LANES
+        ]
+    send(place_x)
+    place_recv[my_chan] = place_send[span(my_chan, rows), :]
 
     arrive(inner_x)
     for row in range(rows):
@@ -360,17 +352,9 @@
     sum_recv[me] = sum_send[...]
 
     arrive(place_x)
-    place_sum[0] = jnp.sum(place_recv[0], axis=0)
+    place_sum[...] = jnp.sum(place_recv[...], axis=0)
     send(spread_x)
-    place_all[span(my_chan, rows), :] = place_sum[0]
-    for num in extras:
-
-        @pl.when(my_chan == 0)
-        def _():
-            arrive(extra_x(num))
-            place_sum[1 + num - chan_count] = jnp.sum(place_recv[1 + num - chan_count], axis=0)
-            send(extra_spread_x(num))
-            place_all[num * rows:(num + 1) * rows, :] = place_sum[1 + num - chan_count]
+    place_all[span(my_chan, rows), :] = place_sum[...]
 
     arrive(slab_x)
     slab = jnp.sum(slab_recv[...], axis=0) * scale
@@ -379,35 +363,29 @@
     skip_grad[...] = exact_dot(jnp.where(picks, 1.0, 0.0).astype(F32), slab, 1, 1)[0:1]
 
     arrive(sum_x)
-    total_recv[span(my_z, part_rows), :] = jnp.sum(sum_recv[...], axis=0) * scale
+    part_row = lax.broadcasted_iota(jnp.int32, (part_rows, LANES), 0) + my_z * part_rows
+    part_lane = lax.broadcasted_iota(jnp.int32, (part_rows, LANES), 1)
+    in_corner = (part_row >= corner) & (part_row < corner + corner_rows) & (part_lane >= hidden)
+    total_recv[span(my_z, part_rows), :] = jnp.where(
+        in_corner, sum_send[...], jnp.sum(sum_recv[...], axis=0) * scale
+    )
     send(total_x)
     for exchange in (pair_x, raw_x, grad_x, inner_x, slab_x, part_x, sum_x, place_x):
         sent(exchange)
 
     arrive(spread_x)
-    for num in extras:
-
-        @pl.when(my_chan == 0)
-        def _():
-            sent(extra_spread_x(num))
-
-        @pl.when(my_chan != 0)
-        def _():
-            for step in chan_steps:
-
-                @pl.when(chan_peer(step)[0] == 0)
-                def _():
-                    copy_of(extra_x(num), step, "own").wait_send()
-                    copy_of(extra_spread_x(num), step, "first").wait_recv()
-
     for row in range(rows):
-        position_grad[:, row * LANES:(row + 1) * LANES] = place_all[
-            pl.ds(row, features, stride=rows), :
+        position_grad[0:chan_count, row * LANES:(row + 1) * LANES] = place_all[
+            pl.ds(row, chan_count, stride=rows), :
         ]
     sent(spread_x)
     arrive(total_x)
     hidden_grad[...] = total_recv[:, 0:hidden]
     embed_grad[...] = total_recv[0:features, hidden:2 * hidden]
+    for num in range(corner_rows):
+        position_grad[chan_count:features, num * hidden:(num + 1) * hidden] = total_recv[
+            corner + num:corner + num + 1, hidden:2 * hidden
+        ]
     sent(total_x)
 
 
@@ -443,9 +421,9 @@
     assert channels == ctx_count and length == z_count * LANES
     row_total = channels * z_count
     part_rows = hidden // z_count
-    extra_count = max(1, features - chan_count)
+    assert features == chan_count + 1 and 2 * hidden == LANES
+    assert (features + 7) // 8 * 8 + length // hidden <= hidden
     vmem = pl.BlockSpec(memory_space=pltpu.VMEM)
-    smem = pl.BlockSpec(memory_space=pltpu.SMEM)
     hbm = pl.BlockSpec(memory_space=pltpu.HBM)
     operands = (
         in_gate,
@@ -456,6 +434,8 @@
         position_table,
         hidden_weight,
         filter_weight.T,
+        decay_rate,
+        skip_gain,
         *(jnp.asarray(table) for table in tables(row_total)),
     )
     block = jax.ShapeDtypeStruct((channels, length), BF16)
@@ -470,7 +450,10 @@
         jax.ShapeDtypeStruct((1, channels), F32),
         jax.ShapeDtypeStruct((features, length), F32),
     )
-    scratch = [pltpu.VMEM(operand.shape, operand.dtype) for operand in operands]
+    scratch = [
+        (pltpu.VMEM if operand.ndim > 1 else pltpu.SMEM)(operand.shape, operand.dtype)
+        for operand in operands
+    ]
     scratch += [
         pltpu.VMEM(shape, F32)
         for shape in (
@@ -489,38 +472,34 @@
             (part_rows, LANES),
             (ctx_count, part_rows, LANES),
             (hidden, LANES),
-            (features * z_count, LANES),
-            (1 + extra_count, chan_count, z_count, LANES),
-            (1 + extra_count, z_count, LANES),
-            (features * z_count, LANES),
+            (chan_count * z_count, LANES),
+            (chan_count, z_count, LANES),
+            (z_count, LANES),
+            (chan_count * z_count, LANES),
         )
     ]
     scratch += [pltpu.SemaphoreType.DMA((INPUTS,))]
     scratch += [
         pltpu.SemaphoreType.DMA((2, count))
-        for count in [ctx_count] * 5 + [chan_count, ctx_count, z_count, chan_count]
-    ]
-    scratch += [
-        pltpu.SemaphoreType.DMA((extra_count, 2, chan_count)),
-        pltpu.SemaphoreType.DMA((2, chan_count)),
-        pltpu.SemaphoreType.DMA((extra_count, 2, chan_count)),
+        for count in [ctx_count] * 5 + [chan_count, ctx_count, z_count, chan_count, chan_count]
     ]
     results = pl.pallas_call(
         functools.partial(kernel, ctx_count, z_count, x_count),
         out_shape=shapes,
-        in_specs=[smem] * 2 + [hbm] * INPUTS,
+        in_specs=[hbm] * INPUTS,
         out_specs=tuple([vmem] * 9),
         scratch_shapes=scratch,
         compiler_params=pltpu.CompilerParams(
-            collective_id=0, has_side_effects=True, vmem_limit_bytes=67043328
+            collective_id=0, has_side_effects=True, vmem_limit_bytes=40 * 1024 * 1024
         ),
-    )(decay_rate, skip_gain, *operands)
+    )(*(pltpu.with_memory_space_constraint(operand, pltpu.HBM) for operand in operands))
     results = pl.pallas_call(
         put_out,
-        out_shape=shapes,
+        out_shape=tuple(pltpu.HBM(shape.shape, shape.dtype) for shape in shapes),
         in_specs=[vmem] * 9,
         out_specs=tuple([hbm] * 9),
         scratch_shapes=[pltpu.SemaphoreType.DMA((9,))],
+        compiler_params=pltpu.CompilerParams(vmem_limit_bytes=4 * 1024 * 1024),
     )(*results)
     results = list(results)
     results[6] = results[6].T

time: 54 us -> 50.4 us (0.933)
  Pallas kernels: 53.2 us -> 49.6 us
    pallas_call x1, Pallas kernels: 51.3 us -> 48.8 us  [shards(): pl.pallas_call(functools.partial(kernel, ctx_count, z_count, x_count), ou...]
    pallas_call x1, Pallas kernels: 1.87 us -> 0.82 us  [shards(): pl.pallas_call(put_out, out_shape=tuple((pltpu.HBM(shape.shape, shape.dty...]
where the time goes in v3:
time: 50.4 us; the launch traced here: 50.3 us
  Pallas kernels  49.6 us (98%)
  between operations  0.65 us (1%)
    pallas_call x1, Pallas kernels, shards(): pl.pallas_call(functools.partial(kernel, ctx_count, z_count, x_count), ou...  48.8 us

profile of v3, /device:TPU:1, one launch (start us, length us, event | category | flops | bytes accessed | tf_op | source)
XLA Modules:
  0.0 50.3 jit_solution(17662121113164004146)
XLA Ops:
  0.6 48.8 %shard_map.214 = (bf16[16,1024]{1,0:T(8,128)(2,1)S(1)}, bf16[16,1024]{1,0:T(8,128)(2,1)S(1)}, bf16[16,1024]{1,0:T(8,128)(2,1)S(1)}, bf16[16,1024]{1,0:T(8,128)(2...) custom-call(bf16[16,1024]{1,0:T(8,128)(2,1)} %refs_0_.1, ...), custom_call_target="tpu_custom_call" | custom-call | tf_op jit(solution)/shard_map/pallas_call | solution.py:486
  49.5 0.8 %shard_map.215 = (bf16[16,1024]{1,0:T(8,128)(2,1)}, bf16[16,1024]{1,0:T(8,128)(2,1)}, bf16[16,1024]{1,0:T(8,128)(2,1)}, bf16[16,1024]{1,0:T(8,128)(2,1)}, f32[33...) custom-call(bf16[16,1024]{1,0:T(8,128)(2,1)S(1)} %get-tuple-element.27.refs_0_, ...), custom_call_target="tpu_custom_call" | custom-call | tf_op jit(solution)/shard_map/pallas_call | solution.py:496

commit v4 on v3

--- a/solution.py
+++ b/solution.py
@@ -101,9 +101,10 @@
      filter_weight, decay, skip, first_ref, last_ref, second_ref, back_ref, twist) = locals_of
     (pair_send, pair_recv, raw_send, raw_recv, grad_send, grad_recv, inner_send, inner_recv,
      slab_send, slab_recv, part_send, part_recv, sum_send, sum_recv, total_recv,
-     place_send, place_recv, place_sum, place_all), refs = refs[:19], refs[19:]
+     place_send, place_recv, place_sum, place_all, act_one_keep, act_two_keep, position_keep,
+     hidden_keep, embed_keep, cos_one_keep, cos_two_keep), refs = refs[:26], refs[26:]
     (load_sems, pair_sems, raw_sems, grad_sems, inner_sems, slab_sems, part_sems, sum_sems,
-     total_sems, place_sems, spread_sems) = refs
+     total_sems, place_sems, spread_sems, round_sems) = refs
 
     chan_count = z_count * x_count
     rows = z_count
@@ -177,6 +178,12 @@
     def sent(exchange):
         for step in exchange[0][2]:
             copy_of(exchange, step, "own").wait_send()
+
+    def both(table):
+        return table[0], table[1]
+
+    def keep_halves(keep, value):
+        keep[0], keep[1] = split(value)
 
     pair_x = (over_ctx, lambda p: pair_send.at[:, span(p, rows), :],
               lambda p: pair_recv.at[:, span(p, rows), :], pair_sems)
@@ -199,12 +206,28 @@
     corner_rows = rows * LANES // hidden
 
     barrier = pltpu.get_barrier_semaphore()
-    for step in chan_steps:
-        pl.semaphore_signal(barrier, inc=1, device_id=chan_peer(step)[1],
-                            device_id_type=pl.DeviceIdType.MESH)
+    z_sides = [ahead(my_z, step, z_count) * x_count + my_x for step in (1, z_count - 1)]
+    x_sides = [my_z * x_count + ahead(my_x, step, x_count) for step in (1, x_count - 1)]
     for step in ctx_steps:
         pl.semaphore_signal(barrier, inc=1, device_id=ctx_peer(step)[1],
                             device_id_type=pl.DeviceIdType.MESH)
+    for side in z_sides + x_sides:
+        pl.semaphore_signal(barrier, inc=1, device_id={"chan": side},
+                            device_id_type=pl.DeviceIdType.MESH)
+
+    round_sides = [z_sides] * (z_count // 2 - 1) + [x_sides] * (x_count // 2)
+
+    def tell(num):
+        for way, side in enumerate(round_sides[num]):
+            pl.semaphore_signal(round_sems.at[num, way], inc=1, device_id={"chan": side},
+                                device_id_type=pl.DeviceIdType.MESH)
+
+    def hear(first, last):
+        for num in range(first, min(last, len(round_sides))):
+            for way in range(2):
+                pl.semaphore_wait(round_sems.at[num, way], 1)
+            if num + 1 < len(round_sides):
+                tell(num + 1)
 
     for num in range(4):
         loads[num].wait()
@@ -222,14 +245,14 @@
     act_one, cos_one = sine_cosine(pre_one)
     pre_two = exact_dot(hidden_weight[...], act_one, 0, 0)
     act_two, cos_two = sine_cosine(pre_two)
-    act_two_halves = split(act_two)
     filter_halves = split(filter_weight[...])
-    raw_filter = pair_dot(filter_halves, act_two_halves, 1, 0)
+    raw_filter = pair_dot(filter_halves, split(act_two), 1, 0)
     for row in range(rows):
         cut = slice(row * LANES, (row + 1) * LANES)
         raw_send[pl.ds(row, channels, stride=rows), :] = raw_filter[:, cut]
 
-    pl.semaphore_wait(barrier, ctx_count + chan_count - 2)
+    pl.semaphore_wait(barrier, ctx_count + 3)
+    tell(0)
     send(pair_x)
     send(raw_x)
     pair_recv[:, span(me, rows), :] = pair_send[:, span(me, rows), :]
@@ -237,12 +260,17 @@
     for num in range(10, INPUTS):
         loads[num].wait()
 
+    keep_halves(act_one_keep, act_one)
+    keep_halves(act_two_keep, act_two)
+    keep_halves(position_keep, position_table[...])
+    keep_halves(hidden_keep, hidden_weight[...])
+    keep_halves(embed_keep, embed_weight[...])
+    cos_one_keep[...] = cos_one
+    cos_two_keep[...] = cos_two
+
     turn_cos = twist[0]
     turn_sin = twist[1]
     row_total = channels * rows
-
-    def both(table):
-        return table[0], table[1]
 
     def forward(fields):
         half = pair_dot(both(first_ref), split(jnp.concatenate(fields, axis=1)), 1, 0)
@@ -279,6 +307,7 @@
     ).astype(F32)
     envelope = jnp.exp(-decay[me] * cells)
 
+    hear(0, 3)
     arrive(pair_x)
     own_product = pair_recv[0]
     own_through = pair_recv[1]
@@ -304,37 +333,38 @@
     send(inner_x)
     inner_recv[:, span(me, rows), :] = inner_send[:, span(me, rows), :]
 
+    hear(3, len(round_sides))
+
     arrive(grad_x)
     raw_grad = jnp.concatenate(
         [grad_recv[pl.ds(row, channels, stride=rows), :] for row in range(rows)], axis=1
     )
     raw_grad_halves = split(raw_grad)
-    pre_two_grad = pair_dot(filter_halves, raw_grad_halves, 0, 0) * cos_two
+    pre_two_grad = pair_dot(filter_halves, raw_grad_halves, 0, 0) * cos_two_keep[...]
     pre_two_halves = split(pre_two_grad)
-    pre_one_grad = pair_dot(split(hidden_weight[...]), pre_two_halves, 1, 0) * cos_one
+    pre_one_grad = pair_dot(both(hidden_keep), pre_two_halves, 1, 0) * cos_one_keep[...]
     pre_one_halves = split(pre_one_grad)
     part_send[...] = jnp.zeros_like(part_send)
-    part_send[:, 0:hidden] = pair_dot(split(act_one), pre_two_halves, 1, 1)
+    part_send[:, 0:hidden] = pair_dot(both(act_one_keep), pre_two_halves, 1, 1)
     part_send[0:features, hidden:2 * hidden] = pair_dot(
-        split(position_table[...]), pre_one_halves, 1, 1
-    )
-    place = pair_dot(split(embed_weight[...]), pre_one_halves, 1, 0)
+        both(position_keep), pre_one_halves, 1, 1
+    )
+    place = pair_dot(both(embed_keep), pre_one_halves, 1, 0)
     for num in range(corner_rows):
         part_send[corner + num:corner + num + 1, hidden:2 * hidden] = place[
             chan_count:features, num * hidden:(num + 1) * hidden
         ]
     send(part_x)
     part_recv[my_chan] = part_send[span(my_z, part_rows), :]
-    slab_send[...] = jnp.broadcast_to(skip_part, (channels, LANES))
-    slab_send[:, 0:hidden] = pair_dot(raw_grad_halves, act_two_halves, 1, 1)
-    send(slab_x)
-    slab_recv[me] = slab_send[...]
     for row in range(rows):
         place_send[pl.ds(row, chan_count, stride=rows), :] = place[
             0:chan_count, row * LANES:(row + 1) * LANES
         ]
     send(place_x)
     place_recv[my_chan] = place_send[span(my_chan, rows), :]
+    slab_send[...] = jnp.broadcast_to(skip_part, (channels, LANES))
+    slab_send[:, 0:hidden] = pair_dot(raw_grad_halves, both(act_two_keep), 1, 1)
+    slab_recv[me] = slab_send[...]
 
     arrive(inner_x)
     for row in range(rows):
@@ -350,17 +380,12 @@
     sum_send[...] = jnp.sum(part_recv[...], axis=0)
     send(sum_x)
     sum_recv[me] = sum_send[...]
+    send(slab_x)
 
     arrive(place_x)
     place_sum[...] = jnp.sum(place_recv[...], axis=0)
     send(spread_x)
     place_all[span(my_chan, rows), :] = place_sum[...]
-
-    arrive(slab_x)
-    slab = jnp.sum(slab_recv[...], axis=0) * scale
-    filter_grad[...] = slab[:, 0:hidden]
-    picks = lax.broadcasted_iota(jnp.int32, (8, LANES), 1) == hidden
-    skip_grad[...] = exact_dot(jnp.where(picks, 1.0, 0.0).astype(F32), slab, 1, 1)[0:1]
 
     arrive(sum_x)
     part_row = lax.broadcasted_iota(jnp.int32, (part_rows, LANES), 0) + my_z * part_rows
@@ -370,8 +395,14 @@
         in_corner, sum_send[...], jnp.sum(sum_recv[...], axis=0) * scale
     )
     send(total_x)
-    for exchange in (pair_x, raw_x, grad_x, inner_x, slab_x, part_x, sum_x, place_x):
+    for exchange in (pair_x, raw_x, grad_x, inner_x, part_x, place_x, sum_x, slab_x):
         sent(exchange)
+
+    arrive(slab_x)
+    slab = jnp.sum(slab_recv[...], axis=0) * scale
+    filter_grad[...] = slab[:, 0:hidden]
+    picks = lax.broadcasted_iota(jnp.int32, (8, LANES), 1) == hidden
+    skip_grad[...] = exact_dot(jnp.where(picks, 1.0, 0.0).astype(F32), slab, 1, 1)[0:1]
 
     arrive(spread_x)
     for row in range(rows):
@@ -478,11 +509,23 @@
             (chan_count * z_count, LANES),
         )
     ]
+    scratch += [
+        pltpu.VMEM((2,) + shape, BF16)
+        for shape in (
+            (hidden, length),
+            (hidden, length),
+            (features, length),
+            (hidden, hidden),
+            (features, hidden),
+        )
+    ]
+    scratch += [pltpu.VMEM((hidden, length), F32)] * 2
     scratch += [pltpu.SemaphoreType.DMA((INPUTS,))]
     scratch += [
         pltpu.SemaphoreType.DMA((2, count))
         for count in [ctx_count] * 5 + [chan_count, ctx_count, z_count, chan_count, chan_count]
     ]
+    scratch += [pltpu.SemaphoreType.REGULAR((z_count // 2 + x_count // 2, 2))]
     results = pl.pallas_call(
         functools.partial(kernel, ctx_count, z_count, x_count),
         out_shape=shapes,

time: 50.4 us -> 48.8 us (0.968)
  Pallas kernels: 49.6 us -> 48 us
    pallas_call x1, Pallas kernels: 48.8 us -> 47.2 us  [shards(): pl.pallas_call(functools.partial(kernel, ctx_count, z_count, x_count), ou...]
where the time goes in v4:
time: 48.8 us; the launch traced here: 48.6 us
  Pallas kernels  48 us (98%)
  between operations  0.65 us (1%)
    pallas_call x1, Pallas kernels, shards(): pl.pallas_call(functools.partial(kernel, ctx_count, z_count, x_count), ou...  47.2 us

profile of v4, /device:TPU:1, one launch (start us, length us, event | category | flops | bytes accessed | tf_op | source)
XLA Modules:
  0.0 48.6 jit_solution(9032021727660072744)
XLA Ops:
  0.6 47.2 %shard_map.214 = (bf16[16,1024]{1,0:T(8,128)(2,1)S(1)}, bf16[16,1024]{1,0:T(8,128)(2,1)S(1)}, bf16[16,1024]{1,0:T(8,128)(2,1)S(1)}, bf16[16,1024]{1,0:T(8,128)(2...) custom-call(bf16[16,1024]{1,0:T(8,128)(2,1)} %refs_0_.1, ...), custom_call_target="tpu_custom_call" | custom-call | tf_op jit(solution)/shard_map/pallas_call | solution.py:529
  47.8 0.8 %shard_map.215 = (bf16[16,1024]{1,0:T(8,128)(2,1)}, bf16[16,1024]{1,0:T(8,128)(2,1)}, bf16[16,1024]{1,0:T(8,128)(2,1)}, bf16[16,1024]{1,0:T(8,128)(2,1)}, f32[33...) custom-call(bf16[16,1024]{1,0:T(8,128)(2,1)S(1)} %get-tuple-element.27.refs_0_, ...), custom_call_target="tpu_custom_call" | custom-call | tf_op jit(solution)/shard_map/pallas_call | solution.py:539

commit v5 on v4

--- a/solution.py
+++ b/solution.py
@@ -206,16 +206,20 @@
     corner_rows = rows * LANES // hidden
 
     barrier = pltpu.get_barrier_semaphore()
-    z_sides = [ahead(my_z, step, z_count) * x_count + my_x for step in (1, z_count - 1)]
-    x_sides = [my_z * x_count + ahead(my_x, step, x_count) for step in (1, x_count - 1)]
+
+    def z_ways(*distances):
+        ways = {way % z_count for far in distances for way in (far, -far)} - {0}
+        return [ahead(my_z, way, z_count) * x_count + my_x for way in sorted(ways)]
+
+    x_sides = [my_z * x_count + ahead(my_x, step, x_count) for step in range(1, x_count)]
+    near_sides = z_ways(1, 2) + x_sides
     for step in ctx_steps:
         pl.semaphore_signal(barrier, inc=1, device_id=ctx_peer(step)[1],
                             device_id_type=pl.DeviceIdType.MESH)
-    for side in z_sides + x_sides:
+    for side in near_sides:
         pl.semaphore_signal(barrier, inc=1, device_id={"chan": side},
                             device_id_type=pl.DeviceIdType.MESH)
-
-    round_sides = [z_sides] * (z_count // 2 - 1) + [x_sides] * (x_count // 2)
+    round_sides = [z_ways(2), x_sides]
 
     def tell(num):
         for way, side in enumerate(round_sides[num]):
@@ -224,7 +228,7 @@
 
     def hear(first, last):
         for num in range(first, min(last, len(round_sides))):
-            for way in range(2):
+            for way in range(len(round_sides[num])):
                 pl.semaphore_wait(round_sems.at[num, way], 1)
             if num + 1 < len(round_sides):
                 tell(num + 1)
@@ -251,7 +255,7 @@
         cut = slice(row * LANES, (row + 1) * LANES)
         raw_send[pl.ds(row, channels, stride=rows), :] = raw_filter[:, cut]
 
-    pl.semaphore_wait(barrier, ctx_count + 3)
+    pl.semaphore_wait(barrier, ctx_count - 1 + len(near_sides))
     tell(0)
     send(pair_x)
     send(raw_x)
@@ -307,7 +311,7 @@
     ).astype(F32)
     envelope = jnp.exp(-decay[me] * cells)
 
-    hear(0, 3)
+    hear(0, 2)
     arrive(pair_x)
     own_product = pair_recv[0]
     own_through = pair_recv[1]
@@ -333,7 +337,7 @@
     send(inner_x)
     inner_recv[:, span(me, rows), :] = inner_send[:, span(me, rows), :]
 
-    hear(3, len(round_sides))
+    hear(2, len(round_sides))
 
     arrive(grad_x)
     raw_grad = jnp.concatenate(
@@ -365,6 +369,7 @@
     slab_send[...] = jnp.broadcast_to(skip_part, (channels, LANES))
     slab_send[:, 0:hidden] = pair_dot(raw_grad_halves, both(act_two_keep), 1, 1)
     slab_recv[me] = slab_send[...]
+    send(slab_x)
 
     arrive(inner_x)
     for row in range(rows):
@@ -380,7 +385,6 @@
     sum_send[...] = jnp.sum(part_recv[...], axis=0)
     send(sum_x)
     sum_recv[me] = sum_send[...]
-    send(slab_x)
 
     arrive(place_x)
     place_sum[...] = jnp.sum(place_recv[...], axis=0)
@@ -525,7 +529,7 @@
         pltpu.SemaphoreType.DMA((2, count))
         for count in [ctx_count] * 5 + [chan_count, ctx_count, z_count, chan_count, chan_count]
     ]
-    scratch += [pltpu.SemaphoreType.REGULAR((z_count // 2 + x_count // 2, 2))]
+    scratch += [pltpu.SemaphoreType.REGULAR((4, max(4, x_count)))]
     results = pl.pallas_call(
         functools.partial(kernel, ctx_count, z_count, x_count),
         out_shape=shapes,

time: 48.8 us -> 48.8 us (level)
  no operation moved by 1% of the time
where the time goes in v5:
time: 48.8 us; the launch traced here: 48.7 us
  Pallas kernels  48 us (98%)
  between operations  0.65 us (1%)
    pallas_call x1, Pallas kernels, shards(): pl.pallas_call(functools.partial(kernel, ctx_count, z_count, x_count), ou...  47.2 us

profile of v5, /device:TPU:1, one launch (start us, length us, event | category | flops | bytes accessed | tf_op | source)
XLA Modules:
  0.0 48.7 jit_solution(1367705299927909131)
XLA Ops:
  0.6 47.2 %shard_map.214 = (bf16[16,1024]{1,0:T(8,128)(2,1)S(1)}, bf16[16,1024]{1,0:T(8,128)(2,1)S(1)}, bf16[16,1024]{1,0:T(8,128)(2,1)S(1)}, bf16[16,1024]{1,0:T(8,128)(2...) custom-call(bf16[16,1024]{1,0:T(8,128)(2,1)} %refs_0_.1, ...), custom_call_target="tpu_custom_call" | custom-call | tf_op jit(solution)/shard_map/pallas_call | solution.py:533
  47.9 0.8 %shard_map.215 = (bf16[16,1024]{1,0:T(8,128)(2,1)}, bf16[16,1024]{1,0:T(8,128)(2,1)}, bf16[16,1024]{1,0:T(8,128)(2,1)}, bf16[16,1024]{1,0:T(8,128)(2,1)}, f32[33...) custom-call(bf16[16,1024]{1,0:T(8,128)(2,1)S(1)} %get-tuple-element.27.refs_0_, ...), custom_call_target="tpu_custom_call" | custom-call | tf_op jit(solution)/shard_map/pallas_call | solution.py:543

commit v6 on v5

--- a/solution.py
+++ b/solution.py
@@ -149,7 +149,10 @@
 
     ctx_steps = far_first(ctx_count)
     z_steps = far_first(z_count)
-    chan_steps = sorted(range(1, chan_count), key=chan_far)
+    chan_steps = sorted(
+        range(1, chan_count),
+        key=lambda step: (-min(step // x_count, z_count - step // x_count), chan_far(step)),
+    )
     over_ctx = (ctx_peer, me, ctx_steps)
     over_chan = (chan_peer, my_chan, chan_steps)
     over_z = (z_peer, my_z, z_steps)

time: 48.8 us -> 49 us (level)
  no operation moved by 1% of the time
where the time goes in v6:
time: 49 us; the launch traced here: 48.9 us
  Pallas kernels  48.3 us (99%)
  between operations  0.65 us (1%)
    pallas_call x1, Pallas kernels, shards(): pl.pallas_call(functools.partial(kernel, ctx_count, z_count, x_count), ou...  47.4 us

profile of v6, /device:TPU:1, one launch (start us, length us, event | category | flops | bytes accessed | tf_op | source)
XLA Modules:
  0.0 48.9 jit_solution(8954142634710237566)
XLA Ops:
  0.6 47.4 %shard_map.214 = (bf16[16,1024]{1,0:T(8,128)(2,1)S(1)}, bf16[16,1024]{1,0:T(8,128)(2,1)S(1)}, bf16[16,1024]{1,0:T(8,128)(2,1)S(1)}, bf16[16,1024]{1,0:T(8,128)(2...) custom-call(bf16[16,1024]{1,0:T(8,128)(2,1)} %refs_0_.1, ...), custom_call_target="tpu_custom_call" | custom-call | tf_op jit(solution)/shard_map/pallas_call | solution.py:536
  48.1 0.8 %shard_map.215 = (bf16[16,1024]{1,0:T(8,128)(2,1)}, bf16[16,1024]{1,0:T(8,128)(2,1)}, bf16[16,1024]{1,0:T(8,128)(2,1)}, bf16[16,1024]{1,0:T(8,128)(2,1)}, f32[33...) custom-call(bf16[16,1024]{1,0:T(8,128)(2,1)S(1)} %get-tuple-element.27.refs_0_, ...), custom_call_target="tpu_custom_call" | custom-call | tf_op jit(solution)/shard_map/pallas_call | solution.py:546
